TPU v7x, 512 devices: a whole 4x8x8 slice. The times are simulated.
512 devices in a mesh: band: 64 (over z, y), mp: 8 (over x, core).
Axes of the slice: x: 4, y: 8, z: 8, core: 2. Of those that a mesh axis runs over, the one named last changes fastest.
Arguments:
- grid_latent: bfloat16 [262144, 1024], P(('band', 'mp')), may hold values from -6 to 6
- grid_gain: float32 [1024], replicated, may hold values from 0.1 to 1.9
- hidden_in: bfloat16 [16384, 1024], P('band'), may hold values from -6 to 6
- hid_gain: float32 [1024], replicated, may hold values from 0.1 to 1.9
- enc_wq: bfloat16 [1024, 1024], P(None, 'mp'), may hold values from -8 to 8
- enc_wk: bfloat16 [1024, 1024], P(None, 'mp'), may hold values from -0.1875 to 0.1875
- enc_wv: bfloat16 [1024, 1024], P(None, 'mp'), may hold values from -0.1875 to 0.1875
- enc_wo: bfloat16 [1024, 1024], P('mp'), may hold values from -0.1875 to 0.1875
- enc_edges: int32 [16384, 32], P('band'), may hold values from 0 to 262143, as said below
- enc_counts: int32 [16384], P('band'), may hold values from 1 to 32
- proc_gain: float32 [1024], replicated, may hold values from 0.1 to 1.9
- proc_wq: bfloat16 [1024, 1024], P(None, 'mp'), may hold values from -8 to 8
- proc_wk: bfloat16 [1024, 1024], P(None, 'mp'), may hold values from -0.25 to 0.25
- proc_wv: bfloat16 [1024, 1024], P(None, 'mp'), may hold values from -0.1875 to 0.1875
- proc_wo: bfloat16 [1024, 1024], P('mp'), may hold values from -0.1875 to 0.1875
Outputs:
- mixed: bfloat16 [16384, 1024], P('band')
Inputs may be any that keep to these rules, and one draw needn't show every extreme that they name: `enc_edges`: node n lies in band b = n // 256; each of its edges references a grid point from b * 4096 - 512 to (b + 1) * 4096 + 511. Slots at or beyond the node's count hold valid grid points as well.
All inputs are finite; a program needn't handle non-finite values.
Results may differ from a plain program's by a relative error of at most 0.02.
Values may be sent and summed in bfloat16 or wider, within the bound.
A program may use at most 64 MiB of HBM per device.

v0:
```python
import jax
import jax.numpy as jnp
from jax import lax
from jax.sharding import PartitionSpec as P

D = 1024
HEADS = 16
WIN = 128


EPSILON = 1e-05


def with_halo(shard, sides, width):
    for axis, dim in sides:
        peers, length = (lax.axis_size(axis), shard.shape[dim])
        up = [(i, (i + 1) % peers) for i in range(peers - 1)]
        down = [(j, i) for i, j in up]
        last = lax.slice_in_dim(shard, length - width, length, axis=dim)
        initial = lax.slice_in_dim(shard, 0, width, axis=dim)
        before = lax.ppermute(last, axis, up)
        after = lax.ppermute(initial, axis, down)
        shard = jnp.concatenate([before, shard, after], axis=dim)
    return shard


def layer_norm(values, gain):
    values = values.astype(jnp.float32)
    center = values - jnp.mean(values, axis=-1, keepdims=True)
    spread = jnp.mean(center * center, axis=-1, keepdims=True)
    return center * lax.rsqrt(spread + EPSILON) * gain


def softmax_rows(scores):
    top = jnp.max(scores, axis=-1, keepdims=True)
    expd = jnp.exp(scores - top)
    return (expd / jnp.sum(expd, axis=-1, keepdims=True)).astype(jnp.bfloat16)


def edge_attention(query, keys, values, valid):
    scale = query.shape[-1] ** (-0.5)
    scores = jnp.einsum("nhe,nshe->nhs", query, keys, preferred_element_type=jnp.float32) * scale
    scores = jnp.where(valid[:, None, :], scores, -jnp.inf)
    weights = softmax_rows(scores)
    out = jnp.einsum("nhs,nshe->nhe", weights, values, preferred_element_type=jnp.float32)
    return out.astype(jnp.bfloat16)


def window_attention(query, keys, values, valid):
    scale = query.shape[-1] ** (-0.5)
    scores = jnp.einsum("nhe,mhe->nhm", query, keys, preferred_element_type=jnp.float32) * scale
    scores = jnp.where(valid[:, None, :], scores, -jnp.inf)
    weights = softmax_rows(scores)
    out = jnp.einsum("nhm,mhe->nhe", weights, values, preferred_element_type=jnp.float32)
    return out.astype(jnp.bfloat16)


def project(rows, weight):
    return jnp.dot(rows, weight, preferred_element_type=jnp.float32).astype(jnp.bfloat16)


def mix_heads(heads, w_out):
    return lax.psum(
        jnp.dot(heads, w_out, preferred_element_type=jnp.float32).astype(jnp.bfloat16), "mp"
    ).astype(jnp.float32)


def shards(
    grid_latent,
    grid_gain,
    hidden_in,
    hid_gain,
    enc_wq,
    enc_wk,
    enc_wv,
    enc_wo,
    enc_edges,
    enc_counts,
    proc_gain,
    proc_wq,
    proc_wk,
    proc_wv,
    proc_wo,
):
    band_index = lax.axis_index("band")
    band_count = lax.axis_size("band")
    columns = enc_wk.shape[1]
    head_dim = D // HEADS
    local_heads = columns // head_dim
    node_rows = hidden_in.shape[0]
    slots = enc_edges.shape[1]
    grid_norm = layer_norm(grid_latent, grid_gain).astype(jnp.bfloat16)
    pair_weight = jnp.stack([enc_wk, enc_wv])
    grid_pair = jnp.einsum(
        "rd,sdc->src",
        lax.all_gather(grid_norm, "mp", axis=0, tiled=True),
        pair_weight,
        preferred_element_type=jnp.float32,
    ).astype(jnp.bfloat16)
    grid_band = grid_pair.shape[1]
    rim_rows = grid_band // 8
    grid_wide = with_halo(grid_pair, (("band", 1),), rim_rows)
    node_norm = layer_norm(hidden_in, hid_gain).astype(jnp.bfloat16)
    enc_query = project(node_norm, enc_wq).reshape(node_rows, local_heads, head_dim)
    first_row = band_index * grid_band - rim_rows
    local_edges = (enc_edges - first_row).reshape(-1)
    near = jnp.take(grid_wide, local_edges, axis=1).reshape(
        2, node_rows, slots, local_heads, head_dim
    )
    valid = jnp.arange(slots, dtype=jnp.int32)[None, :] < enc_counts[:, None]
    enc_heads = edge_attention(enc_query, near[0], near[1], valid).reshape(node_rows, columns)
    latent = hidden_in.astype(jnp.float32) + mix_heads(enc_heads, enc_wo)
    proc_norm = layer_norm(latent, proc_gain).astype(jnp.bfloat16)
    proc_query = project(proc_norm, proc_wq).reshape(node_rows, local_heads, head_dim)
    norm_wide = with_halo(proc_norm, (("band", 0),), WIN)
    keys_wide = project(norm_wide, proc_wk)
    values_wide = project(norm_wide, proc_wv)
    span = node_rows + 2 * WIN
    keys_wide = keys_wide.reshape(span, local_heads, head_dim)
    values_wide = values_wide.reshape(span, local_heads, head_dim)
    start = band_index * node_rows
    own = start + jnp.arange(node_rows, dtype=jnp.int32)
    other = start - WIN + jnp.arange(span, dtype=jnp.int32)
    total = band_count * node_rows
    window_valid = (
        (jnp.abs(own[:, None] - other[None, :]) <= WIN)
        & (other >= 0)[None, :]
        & (other < total)[None, :]
    )
    proc_heads = window_attention(proc_query, keys_wide, values_wide, window_valid).reshape(
        node_rows, columns
    )
    return (latent + mix_heads(proc_heads, proc_wo)).astype(jnp.bfloat16)


def solution(mesh):
    return jax.shard_map(
        shards,
        mesh=mesh,
        in_specs=(
            P(("band", "mp"), None),
            P(),
            P("band", None),
            P(),
            P(None, "mp"),
            P(None, "mp"),
            P(None, "mp"),
            P("mp", None),
            P("band", None),
            P("band"),
            P(),
            P(None, "mp"),
            P(None, "mp"),
            P(None, "mp"),
            P("mp", None),
        ),
        out_specs=P("band", None),
        check_vma=False,
    )
```

profile of v0, /device:TPU:1, one launch (start us, length us, event | category | flops | bytes accessed | tf_op | source)
XLA Modules:
  0.0 448.2 jit_solution(2260836914869664096)
XLA Ops:
  6.5 1.5 convert_reduce_fusion
  8.1 1.7 fusion.14
  9.9 2.2 fusion.16
  13.8 59.3 %all-gather.2.cloned.1.call-done = bf16[4096,1024]{1,0:T(8,128)(2,1)} async-done(((bf16[512,1024]{1,0:T(8,128)(2,1)}), bf16[4096,1024]{1,0:T(8,128)(2,1)}) %all-gather.2.cloned.1.call-update) | async-done | bytes 8388624 | tf_op jit(solution)/shard_map/all_gather | solution.py:96
  73.1 5.8 %fusion.8 = bf16[2,4096,128]{1,2,0:T(8,128)(2,1)S(1)} fusion(bf16[4096,1024]{1,0:T(8,128)(2,1)} %all-gather.2.cloned.1.call-done, bf16[1,1024,128]{1,2,0:T(8,128)(2,1)S(1)} %bitcast.50, bf16[1,1024,128]{1,2,0:T(8,128)(2,1)S(1)} %bitcast.49), kind=kOutput, calls=%fused_computation.10 | convolution fusion | flops 2148794368 | bytes 11010048 | tf_op jit(solution)/shard_map/rd,sdc->src/dot_general | solution.py:94
  79.7 3.1 collective-permute-start
  82.8 1.3 collective-permute-start.1
  85.0 3.5 collective-permute-done
  88.5 3.7 collective-permute-done.1
  92.3 1.7 pad_maximum_fusion
  94.0 5.9 %copy.29 = bf16[2,5120,128]{2,0,1:T(2,128)(2,1)S(1)} copy(bf16[2,5120,128]{1,2,0:T(8,128)(2,1)} %pad_maximum_fusion) | data formatting | bytes 5242880 | tf_op jit(solution)/shard_map/concatenate | solution.py:23
  99.8 53.2 %gather_fusion = bf16[8192,2,128]{2,1,0:T(2,128)(2,1)} fusion(bf16[2,5120,128]{2,0,1:T(2,128)(2,1)S(1)} %copy.29, s32[8192]{0:T(1024)S(1)} %broadcast_clamp_fusion), kind=kCustom, calls=%fused_computation | custom fusion | bytes 8421376 | tf_op jit(solution)/shard_map/jit(_take)/gather | solution.py:107
  153.0 30.1 %fusion.11 = bf16[2,8192,128]{2,0,1:T(2,128)(2,1)S(1)} fusion(bf16[8192,2,128]{2,1,0:T(2,128)(2,1)} %gather_fusion, pred[8192]{0:T(1024)(128)(4,1)S(1)} %compare_and_fusion), kind=kLoop, calls=%fused_computation.13 | loop fusion | flops 2097152 | bytes 8396800 | tf_op jit(solution)/shard_map/jit(_take)/select_n | solution.py:107
  183.1 45.5 %slice_reduce_fusion = (bf16[8192,128]{1,0:T(8,128)(2,1)S(1)}, bf16[8192,128]{1,0:T(8,128)(2,1)}) fusion(bf16[2,8192,128]{2,0,1:T(2,128)(2,1)S(1)} %fusion.11), kind=kLoop, calls=%fused_computation.11 | loop fusion | bytes 8388608 | tf_op jit(solution)/shard_map/slice | solution.py:111
  228.6 8.3 %squeeze.6 = bf16[256,32,2,64]{3,2,1,0:T(2,128)(2,1)} reshape(bf16[8192,128]{1,0:T(8,128)(2,1)} %get-tuple-element.6) | data formatting | bytes 4194304 | tf_op jit(solution)/shard_map/squeeze | solution.py:111
  236.8 12.6 %multiply_reduce_fusion.1 = f32[256,2,32]{1,2,0:T(8,128)} fusion(f32[256,2,64]{2,1,0:T(2,128)S(1)} %copy-done.4, bf16[256,32,2,64]{3,2,1,0:T(2,128)(2,1)} %squeeze.6), kind=kLoop, calls=%fused_computation.7 | loop fusion | flops 3129344 | bytes 2293760
  249.4 3.8 copy.37
  253.3 4.4 copy.47
  257.7 3.2 squeeze.7
  260.9 11.4 %multiply_reduce_fusion = bf16[256,2,64]{2,1,0:T(2,128)(2,1)S(1)} fusion(f32[256,2,32]{1,2,0:T(8,128)} %copy.47, bf16[256,32,2,64]{3,2,1,0:T(2,128)(2,1)} %squeeze.7), kind=kLoop, calls=%fused_computation.6 | loop fusion | flops 3112960 | bytes 2228224
  273.7 71.7 %all-reduce.3.cloned.1.call-done = bf16[256,1024]{1,0:T(8,128)(2,1)} async-done(((bf16[256,1024]{1,0:T(8,128)(2,1)}), bf16[256,1024]{1,0:T(8,128)(2,1)}) %all-reduce.3.cloned.1.call-update) | async-done | bytes 524304 | tf_op jit(solution)/shard_map/psum | solution.py:63
  345.3 1.3 fusion.31
  346.6 1.3 multiply_reduce_fusion.2
  348.0 1.3 multiply_convert_fusion
  349.3 2.5 collective-permute-start.2
  351.7 1.3 collective-permute-start.3
  353.7 1.4 collective-permute-done.2
  355.0 3.8 collective-permute-done.3
  360.5 1.1 convolution_convert_fusion.3
  361.7 1.4 convolution_convert_fusion.4
  364.2 75.4 %all-reduce.5.cloned.1.call-done = bf16[256,1024]{1,0:T(8,128)(2,1)} async-done(((bf16[256,1024]{1,0:T(8,128)(2,1)}), bf16[256,1024]{1,0:T(8,128)(2,1)}) %all-reduce.5.cloned.1.call-update) | async-done | bytes 524304 | tf_op jit(solution)/shard_map/psum | solution.py:63
  439.5 2.1 add_convert_fusion
  (76 shorter events, 8.0 us)
Async XLA Ops:
  6.5 265.9 %copy-start = (bf16[128,1024]{1,0:T(8,128)(2,1)S(1)}, bf16[128,1024]{1,0:T(8,128)(2,1)}, u32[]{:S(2)}) copy-start(bf16[128,1024]{1,0:T(8,128)(2,1)} %param.22) | copy-start | bytes 786436
  6.5 3.3 copy-start.2
  6.5 5.6 %copy-start.9 = (s32[256,32]{0,1:T(8,128)S(1)}, s32[256,32]{0,1:T(8,128)}, u32[]{:S(2)}) copy-start(s32[256,32]{0,1:T(8,128)} %param.23) | copy-start | bytes 98308
  6.5 66.6 %all-gather.2.cloned.1.call-start = ((), (), s32[]{:S(2)}) async-start(), calls=%async_computation | async-start | bytes 9437184 | tf_op jit(solution)/shard_map/all_gather | solution.py:96
  8.1 4.4 copy-start.5
  8.1 4.5 %copy-start.6 = (bf16[1024,128]{1,0:T(8,128)(2,1)S(1)}, bf16[1024,128]{1,0:T(8,128)(2,1)}, u32[]{:S(2)}) copy-start(bf16[1024,128]{1,0:T(8,128)(2,1)} %param.21) | copy-start | bytes 786436
  9.8 3.0 copy-start.1
  9.8 3.5 copy-start.12
  9.8 3.5 copy-start.17
  12.1 333.2 %all-reduce.3.cloned.1.call-start = ((), (), s32[]{:S(2)}) async-start(), calls=%async_computation.1 | async-start | bytes 1048576 | tf_op jit(solution)/shard_map/psum | solution.py:63
  73.1 11.0 %copy-start.11 = (s32[256]{0:T(256)S(1)}, s32[256]{0:T(256)}, u32[]{:S(2)}) copy-start(s32[256]{0:T(256)} %param.24) | copy-start | bytes 3076
  79.7 8.8 %collective-permute-start = (bf16[2,512,128]{1,2,0:T(8,128)(2,1)}, bf16[2,512,128]{1,2,0:T(8,128)(2,1)S(1)}, u32[]{:S(2)}, u32[]{:S(2)}) collective-permute-start(bf16[2,512,128]{1,2,0:T(8,128)(2,1)} %get-tuple-element.7), channel_id=1, source_target_pairs={{0,8},{8,16},{16,24},{24,32},{32,40},{40,48},{48,56},{56,64},{64,7... | collective-permute-start | bytes 786440 | tf_op jit(solution)/shard_map/ppermute | solution.py:21
  82.8 9.4 %collective-permute-start.1 = (bf16[2,512,128]{1,2,0:T(8,128)(2,1)}, bf16[2,512,128]{1,2,0:T(8,128)(2,1)S(1)}, u32[]{:S(2)}, u32[]{:S(2)}) collective-permute-start(bf16[2,512,128]{1,2,0:T(8,128)(2,1)} %get-tuple-element.8), channel_id=1, source_target_pairs={{8,0},{16,8},{24,16},{32,24},{40,32},{48,40},{56,48},{64,56},{72,6... | collective-permute-start | bytes 786440 | tf_op jit(solution)/shard_map/ppermute | solution.py:22
  228.6 8.3 %copy-start.4 = (f32[256,2,64]{2,1,0:T(2,128)S(1)}, f32[256,2,64]{2,1,0:T(2,128)}, u32[]{:S(2)}) copy-start(f32[256,2,64]{2,1,0:T(2,128)} %copy.46) | copy-start | bytes 393220
  272.3 75.6 %copy-start.10 = (f32[1024]{0:T(1024)S(1)}, f32[1024]{0:T(1024)}, u32[]{:S(2)}) copy-start(f32[1024]{0:T(1024)} %param.25) | copy-start | bytes 12292
  273.5 79.8 %copy-start.7 = (bf16[1024,128]{1,0:T(8,128)(2,1)S(1)}, bf16[1024,128]{1,0:T(8,128)(2,1)}, u32[]{:S(2)}) copy-start(bf16[1024,128]{1,0:T(8,128)(2,1)} %param.26) | copy-start | bytes 786436
  273.6 166.0 %all-reduce.5.cloned.1.call-start = ((), (), s32[]{:S(2)}) async-start(), calls=%async_computation.2 | async-start | bytes 1048576 | tf_op jit(solution)/shard_map/psum | solution.py:63
  273.7 85.2 %copy-start.13 = (bf16[1024,128]{1,0:T(8,128)(2,1)S(1)}, bf16[1024,128]{1,0:T(8,128)(2,1)}, u32[]{:S(2)}) copy-start(bf16[1024,128]{1,0:T(8,128)(2,1)} %param.27) | copy-start | bytes 786436
  349.3 5.7 %collective-permute-start.2 = (bf16[128,1024]{1,0:T(8,128)(2,1)S(1)}, bf16[128,1024]{1,0:T(8,128)(2,1)S(1)}, u32[]{:S(2)}, u32[]{:S(2)}) collective-permute-start(bf16[128,1024]{1,0:T(8,128)(2,1)S(1)} %get-tuple-element.9), channel_id=1, source_target_pairs={{0,8},{8,16},{16,24},{24,32},{32,40},{40,48},{48,56},{56,64},{64,7... | collective-permute-start | bytes 786440 | tf_op jit(solution)/shard_map/ppermute | solution.py:21
  351.7 7.1 %collective-permute-start.3 = (bf16[128,1024]{1,0:T(8,128)(2,1)S(1)}, bf16[128,1024]{1,0:T(8,128)(2,1)S(1)}, u32[]{:S(2)}, u32[]{:S(2)}) collective-permute-start(bf16[128,1024]{1,0:T(8,128)(2,1)S(1)} %get-tuple-element.10), channel_id=1, source_target_pairs={{8,0},{16,8},{24,16},{32,24},{40,32},{48,40},{56,48},{64,56},{72,6... | collective-permute-start | bytes 786440 | tf_op jit(solution)/shard_map/ppermute | solution.py:22
  353.7 6.8 %copy-start.14 = (bf16[1024,128]{1,0:T(8,128)(2,1)S(1)}, bf16[1024,128]{1,0:T(8,128)(2,1)}, u32[]{:S(2)}) copy-start(bf16[1024,128]{1,0:T(8,128)(2,1)} %param.28) | copy-start | bytes 786436
  358.9 0.7 copy-start.15
  359.6 0.9 copy-start.16
  361.7 1.4 copy-start.8
  361.7 77.9 %copy-start.3 = (bf16[256,1024]{1,0:T(8,128)(2,1)S(1)}, bf16[256,1024]{1,0:T(8,128)(2,1)}, u32[]{:S(2)}) copy-start(bf16[256,1024]{1,0:T(8,128)(2,1)} %all-reduce.3.cloned.1.call-done) | copy-start | bytes 1572868
Sparse Core Ops, SparseCore 0:
  12.2 60.8 all-gather.1
  273.7 71.5 all-reduce.2
  364.3 75.1 all-reduce.4
where the time goes:
time: 449 us; the launch traced here: 448 us
  waiting for transfers between devices  219 us (49%)
  local copies, waits for them, and re-layouts  127 us (28%)
  other arithmetic  68.1 us (15%)
  between operations  13.5 us (3%)
  matrix products  12.6 us (3%)
  starting transfers between devices  8.24 us (2%)
    psum x2, waiting for transfers between devices, mix_heads(): lax.psum(jnp.dot(heads, w_out, preferred_element_type=jnp.float32).astype...  147 us
    all_gather x1, waiting for transfers between devices, shards(): lax.all_gather(grid_norm, 'mp', axis=0, tiled=True)  59.3 us
    gather x1, local copies, waits for them, and re-layouts, shards(): jnp.take(grid_wide, local_edges, axis=1)  53.2 us
    slice x1, local copies, waits for them, and re-layouts, shards(): near[1]  45.5 us
    select_n x2, other arithmetic, shards(): jnp.take(grid_wide, local_edges, axis=1)  30.2 us
    unnamed x2, other arithmetic  24 us
  transfers between devices with their start and end apart: 7, of which 7 were waited for; matrix products, arithmetic and copies ran while one was open for 1% of the time, Pallas kernels for 0%

commit v1 on v0

v1 whole, which is shorter than its diff:
```python
import functools

import jax
import jax.numpy as jnp
from jax import lax
from jax.experimental import pallas as pl
from jax.experimental.pallas import tpu as pltpu
from jax.sharding import PartitionSpec as P

MESH = pl.DeviceIdType.MESH
EPSILON = 1e-05
NEG = -1e30
F32 = jnp.float32
BF16 = jnp.bfloat16

D = 1024
CHIPS = 4
ROWS = 512
NODES = 256
SLOTS = 32
WIN = 128
COLS = 128
HALF = 64
OWN = NODES // CHIPS


def norm_rows(values, gain):
    values = values.astype(F32)
    center = values - jnp.mean(values, axis=-1, keepdims=True)
    spread = jnp.mean(center * center, axis=-1, keepdims=True)
    return center * lax.rsqrt(spread + EPSILON) * gain


def at_cols(start):
    return pl.ds(pl.multiple_of(start, COLS), COLS)


class Ring:
    def __init__(self, place, own, send, recv):
        self.place, self.own, self.send, self.recv = place, own, send, recv

    def bind(self, x, c):
        self.x, self.c = x, c
        self.left, self.right = lax.rem(x + 3, 4), lax.rem(x + 1, 4)
        self.far = lax.rem(x + 2, 4)
        return self

    def copy(self, source, c, x, half, kind):
        target = (2 * self.right + self.c, 2 * self.left + self.c, 2 * self.x + 1 - self.c)[kind]
        return pltpu.make_async_remote_copy(
            src_ref=source,
            dst_ref=self.place(c, x, half),
            send_sem=self.send.at[kind, x, half],
            recv_sem=self.recv.at[c, x, half],
            device_id={"mp": target},
            device_id_type=MESH,
        )

    def held(self, c, x, half, kind):
        return self.copy(self.place(c, x, half), c, x, half, kind)

    def start(self):
        for half in range(2):
            for kind in range(2):
                self.copy(self.own(half), self.c, self.x, half, kind).start()

    def start_partner(self):
        for half in range(2):
            self.copy(self.own(half), self.c, self.x, half, 2).start()

    def arrived(self, x):
        for half in range(2):
            self.held(self.c, x, half, 2).wait_recv()

    def pass_on(self, x):
        for half in range(2):
            self.held(self.c, x, half, 2).start()

    def relay_left(self, partner):
        self.arrived(self.left)
        self.held(self.c, self.left, 0, 0).start()
        if partner:
            self.pass_on(self.left)

    def relay_right(self, partner):
        self.arrived(self.right)
        self.held(self.c, self.right, 1, 1).start()
        if partner:
            self.pass_on(self.right)

    def relay_far(self, partner):
        self.arrived(self.far)
        if partner:
            self.pass_on(self.far)

    def from_partner(self):
        for x in range(4):
            for half in range(2):
                self.held(1 - self.c, x, half, 2).wait_recv()

    def drain(self, partner):
        for half in range(2):
            for kind in range(2):
                self.copy(self.own(half), self.c, self.x, half, kind).wait_send()
        self.held(self.c, self.left, 0, 0).wait_send()
        self.held(self.c, self.right, 1, 1).wait_send()
        if partner:
            for half in range(2):
                self.copy(self.own(half), self.c, self.x, half, 2).wait_send()
                for x in (self.left, self.right, self.far):
                    self.held(self.c, x, half, 2).wait_send()


def fill_bias(edges_ref, counts_ref, bias_ref, base, width):
    step = 16
    slot = lax.broadcasted_iota(jnp.int32, (step, SLOTS), 1)
    column = lax.broadcasted_iota(jnp.int32, (step, width), 1)
    lane = lax.broadcasted_iota(jnp.int32, (step, NODES), 1)
    row = lax.broadcasted_iota(jnp.int32, (step, NODES), 0)

    def block(i, carry):
        at = pl.multiple_of(i * step, step)
        picked = jnp.where(lane == row + at, counts_ref[...], 0)
        count = jnp.sum(picked, axis=1, keepdims=True)
        edges = jnp.where(slot < count, edges_ref[pl.ds(at, step), :] - base, -1)
        total = jnp.zeros((step, width), F32)
        for s in range(SLOTS):
            total = total + jnp.where(edges[:, s : s + 1] == column, 1.0, 0.0)
        bias_ref[pl.ds(at, step), :] = jnp.where(
            total > 0.0, jnp.log(jnp.maximum(total, 1.0)), NEG
        )
        return carry

    lax.fori_loop(0, NODES // step, block, 0)


def two_heads(query, keys, values, bias):
    first = lax.broadcasted_iota(jnp.int32, query.shape, 1) < HALF
    outs, sums = [], []
    for h in range(2):
        q = jnp.where(first if h == 0 else jnp.logical_not(first), query, jnp.zeros_like(query))
        scores = lax.dot_general(q, keys, (((1,), (1,)), ((), ())), preferred_element_type=F32) + bias
        top = jnp.max(scores, axis=1, keepdims=True)
        weights = jnp.exp(scores - top).astype(BF16)
        both = jnp.dot(weights, values, preferred_element_type=F32)
        total = both[:, COLS:]
        outs.append(both[:, :COLS] / total)
        sums.append(top + jnp.log(total))
    return jnp.where(first, outs[0], outs[1]).astype(BF16), sums


def kernel(
    bands,
    grid, wk, wv, wo, pwk, pwv, pwq, pwo, edges_hbm, counts_hbm,
    grid_gain, hidden, hid_gain, wq, edges, counts, proc_gain,
    out,
    raw, normed, node, w, q, qr, keys, vals, bias, bias_r, edges_r, counts_r,
    part, stat, part_r, stat_r, po, st, heads, wo_all, pwo_all, latent, pw, pq, kvp, heads2,
    ks, kr, vs, vr, os, orr, ps, pr, hs, hr, gs, gr,
    loc, grid_sem, edge_sem, q_send, q_recv, qr_send, qr_recv,
    po_send, po_recv, st_send, st_recv, ro_send, rs_send, kv_send, kv_recv,
):
    b, m = lax.axis_index("band"), lax.axis_index("mp")
    x, c = lax.div(m, 2), lax.rem(m, 2)
    up, down = lax.rem(b + 1, bands), lax.rem(b + bands - 1, bands)
    is_top, is_low = x == 3, x == 0
    is_rim = jnp.logical_or(is_top, is_low)

    barrier = pltpu.get_barrier_semaphore()
    for d in range(1, 8):
        pl.semaphore_signal(barrier, inc=1, device_id={"mp": lax.rem(m + d, 8)}, device_id_type=MESH)
    for band in (up, down):
        for d in range(4):
            pl.semaphore_signal(
                barrier, inc=1, device_id={"band": band, "mp": 2 * d + c}, device_id_type=MESH
            )

    slot = c * 4 + x
    local = [
        pltpu.make_async_copy(wk, w.at[x, :, 0:COLS], loc.at[0]),
        pltpu.make_async_copy(wv, w.at[x, :, COLS:], loc.at[1]),
        pltpu.make_async_copy(grid, raw.at[pl.ds(pl.multiple_of(c * ROWS, ROWS), ROWS), :], loc.at[2]),
        pltpu.make_async_copy(wo, wo_all.at[pl.ds(pl.multiple_of(slot * COLS, COLS), COLS), :], loc.at[3]),
        pltpu.make_async_copy(pwo, pwo_all.at[pl.ds(pl.multiple_of(slot * COLS, COLS), COLS), :], loc.at[4]),
        pltpu.make_async_copy(pwk, pw.at[:, 0:COLS], loc.at[5]),
        pltpu.make_async_copy(pwv, pw.at[:, COLS:], loc.at[6]),
        pltpu.make_async_copy(pwq, pq, loc.at[7]),
    ]
    for one in local:
        one.start()
    pl.semaphore_wait(barrier, 15)

    def rows_of(ref, half):
        return ref.at[pl.ds(half * (D // 2), D // 2), :]

    ring_k = Ring(
        lambda cc, xx, half: w.at[xx, pl.ds(half * (D // 2), D // 2), pl.ds(0, COLS)],
        lambda half: rows_of(wk, half), ks, kr,
    ).bind(x, c)
    ring_v = Ring(
        lambda cc, xx, half: w.at[xx, pl.ds(half * (D // 2), D // 2), pl.ds(COLS, COLS)],
        lambda half: rows_of(wv, half), vs, vr,
    ).bind(x, c)

    def eighth(ref):
        return lambda cc, xx, half: ref.at[
            pl.ds(pl.multiple_of((cc * 4 + xx) * COLS + half * HALF, HALF), HALF), :
        ]

    ring_o = Ring(eighth(wo_all), lambda half: wo.at[pl.ds(half * HALF, HALF), :], os, orr).bind(x, c)
    ring_p = Ring(eighth(pwo_all), lambda half: pwo.at[pl.ds(half * HALF, HALF), :], ps, pr).bind(x, c)

    def head_piece(cc, xx, half):
        return heads.at[
            pl.ds(pl.multiple_of(xx * OWN + half * (OWN // 2), OWN // 2), OWN // 2),
            pl.ds(pl.multiple_of(cc * 512, 512), 512),
        ]

    ring_h = Ring(head_piece, lambda half: head_piece(c, x, half), hs, hr).bind(x, c)

    def out_piece(cc, xx, half):
        return heads2.at[pl.ds(half * 128, 128), at_cols((cc * 4 + xx) * COLS)]

    ring_g = Ring(out_piece, lambda half: out_piece(c, x, half), gs, gr).bind(x, c)

    ring_k.start()
    ring_v.start()
    grid_own = pl.ds(pl.multiple_of(c * ROWS, ROWS), ROWS)
    grid_other = pl.ds(pl.multiple_of((1 - c) * ROWS, ROWS), ROWS)
    to_partner = pltpu.make_async_remote_copy(
        src_ref=grid, dst_ref=raw.at[grid_own, :], send_sem=grid_sem.at[0], recv_sem=grid_sem.at[1],
        device_id={"mp": 2 * x + 1 - c}, device_id_type=MESH,
    )
    to_partner.start()

    def rim_input(source, target, k, band):
        return pltpu.make_async_remote_copy(
            src_ref=source, dst_ref=target, send_sem=edge_sem.at[0, k], recv_sem=edge_sem.at[1, k],
            device_id={"band": band, "mp": m}, device_id_type=MESH,
        )

    rim_from = jnp.where(is_top, down, up)
    rim_to = jnp.where(is_top, up, down)
    edge_copies = [
        rim_input(edges_hbm, edges_r, 0, rim_from),
        rim_input(counts_hbm, counts_r, 1, rim_from),
    ]

    @pl.when(is_rim)
    def _():
        for one in edge_copies:
            one.start()

    def node_block(i, carry):
        at = pl.ds(pl.multiple_of(i * 64, 64), 64)
        node[at, :] = norm_rows(hidden[at, :], hid_gain[...]).astype(BF16)
        return carry

    lax.fori_loop(0, NODES // 64, node_block, 0)
    q[x] = jnp.dot(node[...], wq[...], preferred_element_type=F32).astype(BF16) * BF16(0.125)

    def q_copy(d):
        return pltpu.make_async_remote_copy(
            src_ref=q.at[x], dst_ref=q.at[x], send_sem=q_send.at[d], recv_sem=q_recv.at[x],
            device_id={"mp": 2 * lax.rem(x + d + 1, 4) + c}, device_id_type=MESH,
        )

    def qr_copy(k):
        return pltpu.make_async_remote_copy(
            src_ref=q.at[x], dst_ref=qr.at[x], send_sem=qr_send.at[k], recv_sem=qr_recv.at[x],
            device_id={"band": (down, up)[k], "mp": (6, 0)[k] + c}, device_id_type=MESH,
        )

    def q_arrival(ref, sems, xx):
        return pltpu.make_async_remote_copy(
            src_ref=ref.at[xx], dst_ref=ref.at[xx], send_sem=q_send.at[0], recv_sem=sems.at[xx],
            device_id={"mp": 2 * xx + c}, device_id_type=MESH,
        )

    for d in range(3):
        q_copy(d).start()
    for k in range(2):
        qr_copy(k).start()

    def grid_block(i, carry):
        at = pl.ds(pl.multiple_of(i * 64, 64), 64)
        normed[at, :] = norm_rows(raw[at, :], grid_gain[...]).astype(BF16)
        return carry

    local[2].wait()
    lax.fori_loop(c * 8, c * 8 + 8, grid_block, 0)

    base = b * (8 * ROWS) + x * (2 * ROWS)
    rim_row = jnp.where(is_top, ROWS, 0)
    fill_bias(edges, counts, bias, base, 2 * ROWS)
    vals[:, COLS:] = jnp.ones((2 * ROWS, COLS), BF16)
    stat[...] = jnp.zeros_like(stat)
    stat_r[...] = jnp.zeros_like(stat_r)

    pltpu.make_async_remote_copy(
        src_ref=grid, dst_ref=raw.at[grid_other, :], send_sem=grid_sem.at[0], recv_sem=grid_sem.at[1],
        device_id={"mp": 2 * x + 1 - c}, device_id_type=MESH,
    ).wait_recv()
    lax.fori_loop((1 - c) * 8, (1 - c) * 8 + 8, grid_block, 0)

    @pl.when(is_rim)
    def _():
        for one in edge_copies:
            one.wait_recv()
        fill_bias(edges_r, counts_r, bias_r, base + rim_row, ROWS)

    def part_copy(xs, d):
        xx = lax.rem(x + d + 1, 4)
        return pltpu.make_async_remote_copy(
            src_ref=part.at[xs, pl.ds(pl.multiple_of(xx * OWN, OWN), OWN), :],
            dst_ref=po.at[x, xs],
            send_sem=po_send.at[d, xs], recv_sem=po_recv.at[x, xs],
            device_id={"mp": 2 * xx + c}, device_id_type=MESH,
        )

    rim_slot = jnp.where(is_top, 4, 5)

    def rim_copy(xs, xx):
        return pltpu.make_async_remote_copy(
            src_ref=part_r.at[xs, pl.ds(xx * OWN, OWN), :],
            dst_ref=po.at[rim_slot, xs],
            send_sem=ro_send.at[xx, xs], recv_sem=po_recv.at[rim_slot, xs],
            device_id={"band": rim_to, "mp": 2 * xx + c}, device_id_type=MESH,
        )

    def stat_copy(d):
        xx = lax.rem(x + d + 1, 4)
        return pltpu.make_async_remote_copy(
            src_ref=stat.at[pl.ds(pl.multiple_of(xx * OWN, OWN), OWN), :],
            dst_ref=st.at[x],
            send_sem=st_send.at[d], recv_sem=st_recv.at[x],
            device_id={"mp": 2 * xx + c}, device_id_type=MESH,
        )

    def rim_stat_copy(xx):
        return pltpu.make_async_remote_copy(
            src_ref=stat_r.at[pl.ds(xx * OWN, OWN), :],
            dst_ref=st.at[rim_slot],
            send_sem=rs_send.at[xx], recv_sem=st_recv.at[rim_slot],
            device_id={"band": rim_to, "mp": 2 * xx + c}, device_id_type=MESH,
        )

    chunk = 128

    def attend(xs, q_ref, bias_ref, part_ref, stat_ref, first_row, width):
        def block(i, carry):
            at = pl.ds(pl.multiple_of(i * chunk, chunk), chunk)
            span = pl.ds(pl.multiple_of(first_row, ROWS), width)
            result, sums = two_heads(q_ref[xs, at, :], keys[span, :], vals[span, :], bias_ref[at, :])
            part_ref[xs, at, :] = result
            lane = lax.broadcasted_iota(jnp.int32, (chunk, 128), 1)
            old = stat_ref[at, :]
            old = jnp.where(lane == 2 * xs, sums[0], old)
            stat_ref[at, :] = jnp.where(lane == 2 * xs + 1, sums[1], old)
            return carry

        lax.fori_loop(0, NODES // chunk, block, 0)

    def head_step(j, carry):
        xs = lax.rem(x + jnp.where(j == 0, 0, jnp.where(j == 1, 3, jnp.where(j == 2, 1, 2))), 4)

        @pl.when(j == 0)
        def _():
            local[0].wait()
            local[1].wait()

        @pl.when(j == 1)
        def _():
            for ring in (ring_k, ring_v):
                ring.relay_left(False)
            for ring in (ring_k, ring_v):
                ring.relay_right(False)
            ring_o.start()
            ring_o.start_partner()

        @pl.when(j == 3)
        def _():
            for ring in (ring_k, ring_v):
                ring.relay_far(False)

        @pl.when(j > 0)
        def _():
            q_arrival(q, q_recv, xs).wait_recv()

        def project(i, inner):
            at = pl.ds(pl.multiple_of(i * ROWS, ROWS), ROWS)
            both = jnp.dot(normed[at, :], w[xs], preferred_element_type=F32).astype(BF16)
            keys[at, :] = both[:, :COLS]
            vals[at, 0:COLS] = both[:, COLS:]
            return inner

        lax.fori_loop(0, 2, project, 0)

        @pl.when(is_rim)
        def _():
            q_arrival(qr, qr_recv, xs).wait_recv()
            attend(xs, qr, bias_r, part_r, stat_r, rim_row, ROWS)
            for xx in range(4):
                rim_copy(xs, xx).start()

        attend(xs, q, bias, part, stat, 0, 2 * ROWS)
        for d in range(3):
            part_copy(xs, d).start()
        return carry

    lax.fori_loop(0, 4, head_step, 0)

    for d in range(3):
        stat_copy(d).start()

    @pl.when(is_rim)
    def _():
        for xx in range(4):
            rim_stat_copy(xx).start()

    mine = pl.ds(pl.multiple_of(x * OWN, OWN), OWN)
    st[x] = stat[mine, :]
    for xs in range(4):
        po[x, xs] = part[xs, mine, :]
    ring_o.relay_left(True)
    ring_o.relay_right(True)

    def arrivals(i):
        for xs in range(4):
            pltpu.make_async_remote_copy(
                src_ref=po.at[i, xs], dst_ref=po.at[i, xs],
                send_sem=po_send.at[0, xs], recv_sem=po_recv.at[i, xs],
                device_id={"mp": m}, device_id_type=MESH,
            ).wait_recv()
        pltpu.make_async_remote_copy(
            src_ref=st.at[i], dst_ref=st.at[i], send_sem=st_send.at[0], recv_sem=st_recv.at[i],
            device_id={"mp": m}, device_id_type=MESH,
        ).wait_recv()

    for d in range(3):
        arrivals(lax.rem(x + d + 1, 4))
    arrivals(4)
    arrivals(5)

    top = st[0]
    for i in range(1, 6):
        top = jnp.maximum(top, st[i])
    shares = [jnp.exp(st[i] - top) for i in range(6)]
    whole = shares[0]
    for i in range(1, 6):
        whole = whole + shares[i]
    shares = [one / whole for one in shares]
    first = lax.broadcasted_iota(jnp.int32, (OWN, COLS), 1) < HALF
    for xs in range(4):
        total = jnp.zeros((OWN, COLS), F32)
        for i in range(6):
            left = jnp.broadcast_to(shares[i][:, 2 * xs : 2 * xs + 1], (OWN, COLS))
            right = jnp.broadcast_to(shares[i][:, 2 * xs + 1 : 2 * xs + 2], (OWN, COLS))
            total = total + jnp.where(first, left, right) * po[i, xs].astype(F32)
        heads[mine, at_cols(c * 512 + xs * COLS)] = total.astype(BF16)

    ring_h.start()
    ring_h.start_partner()
    ring_h.relay_left(True)
    ring_h.relay_right(True)
    ring_h.relay_far(True)
    ring_p.start()
    ring_p.start_partner()
    ring_o.relay_far(True)
    local[3].wait()
    ring_o.from_partner()
    ring_h.from_partner()

    def latent_block(n, carry):
        at = pl.ds(pl.multiple_of(n * 256, 256), 256)
        latent[:, at] = hidden[:, at].astype(F32) + jnp.dot(
            heads[...], wo_all[:, at], preferred_element_type=F32
        )
        return carry

    lax.fori_loop(0, 4, latent_block, 0)

    def latent_norm(i, carry):
        at = pl.ds(pl.multiple_of(i * 64, 64), 64)
        node[at, :] = norm_rows(latent[at, :], proc_gain[...]).astype(BF16)
        return carry

    lax.fori_loop(0, NODES // 64, latent_norm, 0)

    local[5].wait()
    local[6].wait()
    kvp[WIN : WIN + NODES, :] = jnp.dot(
        node[...], pw[...], preferred_element_type=F32
    ).astype(BF16)

    def kv_copy(k):
        source, target = ((NODES, 0), (WIN, WIN + NODES))[k]
        return pltpu.make_async_remote_copy(
            src_ref=kvp.at[pl.ds(source, WIN), :], dst_ref=kvp.at[pl.ds(target, WIN), :],
            send_sem=kv_send.at[k], recv_sem=kv_recv.at[k],
            device_id={"band": (up, down)[k], "mp": m}, device_id_type=MESH,
        )

    for k in range(2):
        kv_copy(k).start()
    local[7].wait()
    query = jnp.dot(node[...], pq[...], preferred_element_type=F32).astype(BF16) * BF16(0.125)
    ring_p.relay_left(True)
    ring_p.relay_right(True)
    for k in range(2):
        kv_copy(k).wait_recv()

    span = NODES + 2 * WIN
    vals[0:span, 0:COLS] = kvp[:, COLS:]
    i = lax.broadcasted_iota(jnp.int32, (NODES, span), 0)
    j = lax.broadcasted_iota(jnp.int32, (NODES, span), 1)
    other = b * NODES - WIN + j
    valid = (jnp.abs(i + WIN - j) <= WIN) & (other >= 0) & (other < bands * NODES)
    result, _ = two_heads(query, kvp[:, 0:COLS], vals[0:span, :], jnp.where(valid, 0.0, NEG))
    heads2[:, at_cols(slot * COLS)] = result

    ring_g.start()
    ring_g.start_partner()
    ring_g.relay_left(True)
    ring_g.relay_right(True)
    ring_g.relay_far(True)
    ring_p.relay_far(True)
    local[4].wait()
    ring_p.from_partner()
    ring_g.from_partner()

    def mixed_block(n, carry):
        at = pl.ds(pl.multiple_of(n * 256, 256), 256)
        out[:, at] = (
            latent[:, at] + jnp.dot(heads2[...], pwo_all[:, at], preferred_element_type=F32)
        ).astype(BF16)
        return carry

    lax.fori_loop(0, 4, mixed_block, 0)

    for ring in (ring_k, ring_v):
        ring.drain(False)
    for ring in (ring_o, ring_p, ring_h, ring_g):
        ring.drain(True)
    to_partner.wait_send()
    for d in range(3):
        q_copy(d).wait_send()
        stat_copy(d).wait_send()
        for xs in range(4):
            part_copy(xs, d).wait_send()
    for k in range(2):
        qr_copy(k).wait_send()
        kv_copy(k).wait_send()

    @pl.when(is_rim)
    def _():
        for one in edge_copies:
            one.wait_send()
        for xx in range(4):
            rim_stat_copy(xx).wait_send()
            for xs in range(4):
                rim_copy(xs, xx).wait_send()


def solution(mesh):
    bands = mesh.shape["band"]

    def step(
        grid_latent, grid_gain, hidden_in, hid_gain, enc_wq, enc_wk, enc_wv, enc_wo,
        enc_edges, enc_counts, proc_gain, proc_wq, proc_wk, proc_wv, proc_wo,
    ):
        counts = enc_counts.reshape(1, NODES)
        hbm = pl.BlockSpec(memory_space=pl.ANY)
        vmem = pl.BlockSpec(memory_space=pltpu.VMEM)
        dma = pltpu.SemaphoreType.DMA
        ring_sems = [dma((3, 4, 2)), dma((2, 4, 2))]
        return pl.pallas_call(
            functools.partial(kernel, bands),
            out_shape=jax.ShapeDtypeStruct((NODES, D), BF16),
            in_specs=[hbm] * 10 + [vmem] * 7,
            out_specs=vmem,
            scratch_shapes=[
                pltpu.VMEM((2 * ROWS, D), BF16),
                pltpu.VMEM((2 * ROWS, D), BF16),
                pltpu.VMEM((NODES, D), BF16),
                pltpu.VMEM((4, D, 2 * COLS), BF16),
                pltpu.VMEM((4, NODES, COLS), BF16),
                pltpu.VMEM((4, NODES, COLS), BF16),
                pltpu.VMEM((2 * ROWS, COLS), BF16),
                pltpu.VMEM((2 * ROWS, 2 * COLS), BF16),
                pltpu.VMEM((NODES, 2 * ROWS), F32),
                pltpu.VMEM((NODES, ROWS), F32),
                pltpu.VMEM((NODES, SLOTS), jnp.int32),
                pltpu.VMEM((1, NODES), jnp.int32),
                pltpu.VMEM((4, NODES, COLS), BF16),
                pltpu.VMEM((NODES, 128), F32),
                pltpu.VMEM((4, NODES, COLS), BF16),
                pltpu.VMEM((NODES, 128), F32),
                pltpu.VMEM((6, 4, OWN, COLS), BF16),
                pltpu.VMEM((6, OWN, 128), F32),
                pltpu.VMEM((NODES, D), BF16),
                pltpu.VMEM((D, D), BF16),
                pltpu.VMEM((D, D), BF16),
                pltpu.VMEM((NODES, D), F32),
                pltpu.VMEM((D, 2 * COLS), BF16),
                pltpu.VMEM((D, COLS), BF16),
                pltpu.VMEM((NODES + 2 * WIN, 2 * COLS), BF16),
                pltpu.VMEM((NODES, D), BF16),
            ]
            + ring_sems * 6
            + [
                dma((8,)),
                dma((2,)),
                dma((2, 2)),
                dma((3,)), dma((4,)),
                dma((2,)), dma((4,)),
                dma((3, 4)), dma((6, 4)),
                dma((3,)), dma((6,)),
                dma((4, 4)), dma((4,)),
                dma((2,)), dma((2,)),
            ],
            compiler_params=pltpu.CompilerParams(
                collective_id=0, has_side_effects=True, vmem_limit_bytes=60 * 1024 * 1024
            ),
        )(
            grid_latent, enc_wk, enc_wv, enc_wo, proc_wk, proc_wv, proc_wq, proc_wo, enc_edges, counts,
            grid_gain.reshape(1, D), hidden_in, hid_gain.reshape(1, D), enc_wq, enc_edges, counts,
            proc_gain.reshape(1, D),
        )

    return jax.shard_map(
        step,
        mesh=mesh,
        in_specs=(
            P(("band", "mp"), None), P(), P("band", None), P(),
            P(None, "mp"), P(None, "mp"), P(None, "mp"), P("mp", None),
            P("band", None), P("band"), P(),
            P(None, "mp"), P(None, "mp"), P(None, "mp"), P("mp", None),
        ),
        out_specs=P("band", None),
        check_vma=False,
    )
```

time: 449 us -> 91.5 us (0.20)
  waiting for transfers between devices: 219 us -> 0 us
  local copies, waits for them, and re-layouts: 127 us -> 3.38 us
  Pallas kernels: 0 us -> 87.9 us
  other arithmetic: 68.1 us -> 0 us
  between operations: 13.5 us -> 0.01 us
  matrix products: 12.6 us -> 0 us
  starting transfers between devices: 8.24 us -> 0 us
    psum x2 -> x0, waiting for transfers between devices: 147 us -> none  [mix_heads(): lax.psum(jnp.dot(heads, w_out, preferred_element_type=jnp.float32).astype...]
    pallas_call x0 -> x1, Pallas kernels: none -> 87.9 us  [step(): pl.pallas_call(functools.partial(kernel, bands), out_shape=jax.ShapeDtype...]
    all_gather x1 -> x0, waiting for transfers between devices: 59.3 us -> none  [shards(): lax.all_gather(grid_norm, 'mp', axis=0, tiled=True)]
    gather x1 -> x0, local copies, waits for them, and re-layouts: 53.2 us -> none  [shards(): jnp.take(grid_wide, local_edges, axis=1)]
    slice x3 -> x0, local copies, waits for them, and re-layouts: 46.3 us -> none  [the longest x1 45.5 us: shards(): near[1]]
    select_n x2 -> x0, other arithmetic: 30.2 us -> none  [shards(): jnp.take(grid_wide, local_edges, axis=1)]
    unnamed x2 -> x0, other arithmetic: 24 us -> none
    ppermute x4 -> x0, waiting for transfers between devices: 12.5 us -> none  [the longest x2 7.57 us: with_halo(): after = lax.ppermute(initial, axis, down)]
  transfers between devices with their start and end apart: 7 -> 0, of which waited for: 7 -> 0; matrix products, arithmetic and copies ran while one was open for 1% -> 0% of each run, Pallas kernels for 0% -> 0%
where the time goes in v1:
time: 91.5 us; the launch traced here: 91.3 us
  Pallas kernels  87.9 us (96%)
  local copies, waits for them, and re-layouts  3.38 us (4%)
    pallas_call x1, Pallas kernels, step(): pl.pallas_call(functools.partial(kernel, bands), out_shape=jax.ShapeDtype...  87.9 us
    unnamed x2, local copies, waits for them, and re-layouts  3.38 us

profile of v1, /device:TPU:1, one launch (start us, length us, event | category | flops | bytes accessed | tf_op | source)
XLA Modules:
  0.0 91.3 jit_solution(6122817457267334796)
XLA Ops:
  0.0 1.5 %copy.16.edges_hbm.edges = s32[256,32]{1,0:T(8,128)} copy(s32[256,32]{0,1:T(8,128)} %param.23) | data formatting | bytes 65536 | tf_op args[8]
  1.5 87.9 %shard_map.145 = bf16[256,1024]{1,0:T(8,128)(2,1)} custom-call(bf16[512,1024]{1,0:T(8,128)(2,1)} %grid.1, bf16[1024,128]{1,0:T(8,128)(2,1)} %wk.1, bf16[1024,128]{1,0:T(8,128)(2,1)} %wv.1, bf16[128,1024]{1,0:T(8,128)(2,1)} %wo.1, bf16[1024,128]{1,0:T(8,128)(2,1)} %pwk.1, bf16[1024,128]{1,0:T(8,128)(2,1)} %pwv.1, bf16[1024,128]{1,0:T(8,128)(2,1)} %pwq.1, ...), custom_call_target="tpu_custom_call" | custom-call | tf_op jit(solution)/shard_map/pallas_call | solution.py:577
  89.4 1.9 %copy.19 = bf16[256,1024]{1,0:T(8,128)(2,1)} copy(bf16[256,1024]{1,0:T(8,128)(2,1)} %shard_map.145) | data formatting | bytes 1048576

commit v2 on v1

--- a/solution.py
+++ b/solution.py
@@ -22,6 +22,7 @@
 COLS = 128
 HALF = 64
 OWN = NODES // CHIPS
+RING = 8
 
 
 def norm_rows(values, gain):
@@ -36,93 +37,130 @@
 
 
 class Ring:
-    def __init__(self, place, own, send, recv):
-        self.place, self.own, self.send, self.recv = place, own, send, recv
-
-    def bind(self, x, c):
-        self.x, self.c = x, c
-        self.left, self.right = lax.rem(x + 3, 4), lax.rem(x + 1, 4)
-        self.far = lax.rem(x + 2, 4)
-        return self
-
-    def copy(self, source, c, x, half, kind):
-        target = (2 * self.right + self.c, 2 * self.left + self.c, 2 * self.x + 1 - self.c)[kind]
-        return pltpu.make_async_remote_copy(
-            src_ref=source,
-            dst_ref=self.place(c, x, half),
-            send_sem=self.send.at[kind, x, half],
-            recv_sem=self.recv.at[c, x, half],
-            device_id={"mp": target},
-            device_id_type=MESH,
-        )
-
-    def held(self, c, x, half, kind):
-        return self.copy(self.place(c, x, half), c, x, half, kind)
+    def __init__(self, place, send, recv, x, c):
+        self.place, self.send, self.recv, self.x, self.c = place, send, recv, x, c
+        self.others = [lax.rem(x + d, 4) for d in (3, 1, 2)]
+
+    def copy(self, c, x, kind, device):
+        ref = self.place(c, x)
+        return pltpu.make_async_remote_copy(
+            src_ref=ref, dst_ref=ref, send_sem=self.send.at[kind], recv_sem=self.recv.at[c, x],
+            device_id={"mp": device}, device_id_type=MESH,
+        )
+
+    def sends(self):
+        return [self.copy(self.c, self.x, k, 2 * xx + self.c) for k, xx in enumerate(self.others)]
+
+    def to_partner(self, k):
+        xx = self.x if k == 3 else self.others[k]
+        return self.copy(self.c, xx, 3 + k, 2 * self.x + 1 - self.c)
 
     def start(self):
-        for half in range(2):
-            for kind in range(2):
-                self.copy(self.own(half), self.c, self.x, half, kind).start()
-
-    def start_partner(self):
-        for half in range(2):
-            self.copy(self.own(half), self.c, self.x, half, 2).start()
-
-    def arrived(self, x):
-        for half in range(2):
-            self.held(self.c, x, half, 2).wait_recv()
-
-    def pass_on(self, x):
-        for half in range(2):
-            self.held(self.c, x, half, 2).start()
-
-    def relay_left(self, partner):
-        self.arrived(self.left)
-        self.held(self.c, self.left, 0, 0).start()
-        if partner:
-            self.pass_on(self.left)
-
-    def relay_right(self, partner):
-        self.arrived(self.right)
-        self.held(self.c, self.right, 1, 1).start()
-        if partner:
-            self.pass_on(self.right)
-
-    def relay_far(self, partner):
-        self.arrived(self.far)
-        if partner:
-            self.pass_on(self.far)
+        for one in self.sends():
+            one.start()
+        self.to_partner(3).start()
+
+    def relay(self):
+        for k, xx in enumerate(self.others):
+            self.copy(self.c, xx, k, 2 * xx + self.c).wait_recv()
+            self.to_partner(k).start()
 
     def from_partner(self):
-        for x in range(4):
-            for half in range(2):
-                self.held(1 - self.c, x, half, 2).wait_recv()
-
-    def drain(self, partner):
-        for half in range(2):
-            for kind in range(2):
-                self.copy(self.own(half), self.c, self.x, half, kind).wait_send()
-        self.held(self.c, self.left, 0, 0).wait_send()
-        self.held(self.c, self.right, 1, 1).wait_send()
-        if partner:
-            for half in range(2):
-                self.copy(self.own(half), self.c, self.x, half, 2).wait_send()
-                for x in (self.left, self.right, self.far):
-                    self.held(self.c, x, half, 2).wait_send()
-
-
-def fill_bias(edges_ref, counts_ref, bias_ref, base, width):
+        for xx in range(4):
+            self.copy(1 - self.c, xx, 0, 2 * self.x + 1 - self.c).wait_recv()
+
+    def drain(self):
+        for one in self.sends():
+            one.wait_send()
+        for k in range(4):
+            self.to_partner(k).wait_send()
+
+
+class Spread:
+    def __init__(self, source, held, n, index, band_of, x, c, m, sems):
+        self.source, self.held, self.n, self.index, self.band_of = source, held, n, index, band_of
+        self.x, self.c, self.m = x, c, m
+        self.x_send, self.x_recv, self.r_send, self.r_recv, self.p_sem = sems
+        self.others = [lax.rem(x + d, 4) for d in (3, 1, 2)]
+        self.rows = COLS // n
+
+    def at(self, i):
+        return pl.ds(pl.multiple_of(i * self.rows, self.rows), self.rows)
+
+    def over_x(self, k):
+        return pltpu.make_async_remote_copy(
+            src_ref=self.source.at[self.at(self.index), :],
+            dst_ref=self.held.at[self.c * 4 + self.x, self.at(self.index), :],
+            send_sem=self.x_send.at[k], recv_sem=self.x_recv.at[self.x],
+            device_id={"mp": 2 * self.others[k] + self.c}, device_id_type=MESH,
+        )
+
+    def piece(self, k, i, sem, recv, band):
+        ref = self.held.at[self.c * 4 + self.others[k], self.at(i), :]
+        return pltpu.make_async_remote_copy(
+            src_ref=ref, dst_ref=ref, send_sem=sem, recv_sem=recv,
+            device_id={"band": band, "mp": self.m}, device_id_type=MESH,
+        )
+
+    def along(self, k, d):
+        i = lax.rem(self.index + d, self.n)
+        return self.piece(
+            k, self.index, self.r_send.at[k, d], self.r_recv.at[self.others[k], self.index], self.band_of(i)
+        )
+
+    def start(self):
+        for k in range(3):
+            self.over_x(k).start()
+
+    def spread(self):
+        for k in range(3):
+            self.piece(
+                k, self.index, self.r_send.at[k, 0], self.x_recv.at[self.others[k]], self.band_of(self.index)
+            ).wait_recv()
+        for d in range(1, self.n):
+            for k in range(3):
+                self.along(k, d).start()
+
+    def to_partner(self, c):
+        ref = self.held.at[pl.ds(c * 4, 4)]
+        return pltpu.make_async_remote_copy(
+            src_ref=ref, dst_ref=ref, send_sem=self.p_sem.at[0], recv_sem=self.p_sem.at[1],
+            device_id={"mp": 2 * self.x + 1 - self.c}, device_id_type=MESH,
+        )
+
+    def collect(self):
+        for k in range(3):
+            for d in range(1, self.n):
+                i = lax.rem(self.index + d, self.n)
+                self.piece(
+                    k, i, self.r_send.at[k, 0], self.r_recv.at[self.others[k], i], self.band_of(i)
+                ).wait_recv()
+        self.to_partner(self.c).start()
+
+    def from_partner(self):
+        self.to_partner(1 - self.c).wait_recv()
+
+    def drain(self):
+        for k in range(3):
+            self.over_x(k).wait_send()
+            for d in range(1, self.n):
+                self.along(k, d).wait_send()
+        self.to_partner(self.c).wait_send()
+
+
+def sort_edges(edges_ref, counts_ref, columns_ref, base):
+    slot = lax.broadcasted_iota(jnp.int32, (SLOTS, NODES), 0)
+    live = jnp.where(slot < counts_ref[...], edges_ref[...] - base, -1).astype(F32)
+    columns_ref[...] = jnp.concatenate([live, jnp.full((COLS - SLOTS, NODES), -1.0, F32)], axis=0).T
+
+
+def fill_bias(columns_ref, bias_ref, width, begin, end):
     step = 16
-    slot = lax.broadcasted_iota(jnp.int32, (step, SLOTS), 1)
-    column = lax.broadcasted_iota(jnp.int32, (step, width), 1)
-    lane = lax.broadcasted_iota(jnp.int32, (step, NODES), 1)
-    row = lax.broadcasted_iota(jnp.int32, (step, NODES), 0)
+    column = lax.broadcasted_iota(jnp.int32, (step, width), 1).astype(F32)
 
     def block(i, carry):
         at = pl.multiple_of(i * step, step)
-        picked = jnp.where(lane == row + at, counts_ref[...], 0)
-        count = jnp.sum(picked, axis=1, keepdims=True)
-        edges = jnp.where(slot < count, edges_ref[pl.ds(at, step), :] - base, -1)
+        edges = columns_ref[pl.ds(at, step), :]
         total = jnp.zeros((step, width), F32)
         for s in range(SLOTS):
             total = total + jnp.where(edges[:, s : s + 1] == column, 1.0, 0.0)
@@ -131,7 +169,7 @@
         )
         return carry
 
-    lax.fori_loop(0, NODES // step, block, 0)
+    lax.fori_loop(begin // step, end // step, block, 0)
 
 
 def two_heads(query, keys, values, bias):
@@ -150,13 +188,14 @@
 
 
 def kernel(
-    bands,
+    bands, ring,
     grid, wk, wv, wo, pwk, pwv, pwq, pwo, edges_hbm, counts_hbm,
     grid_gain, hidden, hid_gain, wq, edges, counts, proc_gain,
     out,
-    raw, normed, node, w, q, qr, keys, vals, bias, bias_r, edges_r, counts_r,
+    raw, normed, node, w, q, qr, keys, vals, bias, bias_r, edges_r, counts_r, columns,
     part, stat, part_r, stat_r, po, st, heads, wo_all, pwo_all, latent, pw, pq, kvp, heads2,
-    ks, kr, vs, vr, os, orr, ps, pr, hs, hr, gs, gr,
+    wx_send, wx_recv, wy_send, wy_recv,
+    o0, o1, o2, o3, o4, p0, p1, p2, p3, p4, hs, hr, gs, gr,
     loc, grid_sem, edge_sem, q_send, q_recv, qr_send, qr_recv,
     po_send, po_recv, st_send, st_recv, ro_send, rs_send, kv_send, kv_recv,
 ):
@@ -166,65 +205,108 @@
     is_top, is_low = x == 3, x == 0
     is_rim = jnp.logical_or(is_top, is_low)
 
+    layers = bands // ring
+    y, z = lax.rem(b, ring), lax.div(b, ring)
+    parity = lax.rem(y, 2)
+
+    def band_in_y(i):
+        return z * ring + i
+
+    def band_in_z(i):
+        return i * ring + y
+
+    ahead, behind = band_in_y(lax.rem(y + 1, ring)), band_in_y(lax.rem(y + ring - 1, ring))
+
     barrier = pltpu.get_barrier_semaphore()
+
+    def greet(device):
+        pl.semaphore_signal(barrier, inc=1, device_id=device, device_id_type=MESH)
+
     for d in range(1, 8):
-        pl.semaphore_signal(barrier, inc=1, device_id={"mp": lax.rem(m + d, 8)}, device_id_type=MESH)
+        greet({"mp": lax.rem(m + d, 8)})
     for band in (up, down):
         for d in range(4):
-            pl.semaphore_signal(
-                barrier, inc=1, device_id={"band": band, "mp": 2 * d + c}, device_id_type=MESH
-            )
+            greet({"band": band, "mp": 2 * d + c})
+    for d in range(1, ring):
+        greet({"band": band_in_y(lax.rem(y + d, ring)), "mp": m})
+    for d in range(1, layers):
+        greet({"band": band_in_z(lax.rem(z + d, layers)), "mp": m})
 
     slot = c * 4 + x
     local = [
         pltpu.make_async_copy(wk, w.at[x, :, 0:COLS], loc.at[0]),
         pltpu.make_async_copy(wv, w.at[x, :, COLS:], loc.at[1]),
         pltpu.make_async_copy(grid, raw.at[pl.ds(pl.multiple_of(c * ROWS, ROWS), ROWS), :], loc.at[2]),
-        pltpu.make_async_copy(wo, wo_all.at[pl.ds(pl.multiple_of(slot * COLS, COLS), COLS), :], loc.at[3]),
-        pltpu.make_async_copy(pwo, pwo_all.at[pl.ds(pl.multiple_of(slot * COLS, COLS), COLS), :], loc.at[4]),
+        pltpu.make_async_copy(wo, wo_all.at[slot], loc.at[3]),
+        pltpu.make_async_copy(pwo, pwo_all.at[slot], loc.at[4]),
         pltpu.make_async_copy(pwk, pw.at[:, 0:COLS], loc.at[5]),
         pltpu.make_async_copy(pwv, pw.at[:, COLS:], loc.at[6]),
         pltpu.make_async_copy(pwq, pq, loc.at[7]),
     ]
     for one in local:
         one.start()
-    pl.semaphore_wait(barrier, 15)
-
-    def rows_of(ref, half):
-        return ref.at[pl.ds(half * (D // 2), D // 2), :]
-
-    ring_k = Ring(
-        lambda cc, xx, half: w.at[xx, pl.ds(half * (D // 2), D // 2), pl.ds(0, COLS)],
-        lambda half: rows_of(wk, half), ks, kr,
-    ).bind(x, c)
-    ring_v = Ring(
-        lambda cc, xx, half: w.at[xx, pl.ds(half * (D // 2), D // 2), pl.ds(COLS, COLS)],
-        lambda half: rows_of(wv, half), vs, vr,
-    ).bind(x, c)
-
-    def eighth(ref):
-        return lambda cc, xx, half: ref.at[
-            pl.ds(pl.multiple_of((cc * 4 + xx) * COLS + half * HALF, HALF), HALF), :
+    pl.semaphore_wait(barrier, 13 + ring + layers)
+
+    others = [lax.rem(x + d, 4) for d in (3, 1, 2)]
+
+    def weight_part(xx, mat, row, count):
+        return w.at[xx, pl.ds(pl.multiple_of(row, 128), count), pl.ds(mat * COLS, COLS)]
+
+    def weight_x(mat, k, s):
+        row = parity * 512 + s * 256
+        return pltpu.make_async_remote_copy(
+            src_ref=(wk, wv)[mat].at[pl.ds(pl.multiple_of(row, 256), 256), :],
+            dst_ref=weight_part(x, mat, row, 256),
+            send_sem=wx_send.at[mat, k, s], recv_sem=wx_recv.at[mat, x, s],
+            device_id={"mp": 2 * others[k] + c}, device_id_type=MESH,
+        )
+
+    def weight_y(mat, k, s, t, half):
+        ref = weight_part(others[k], mat, half * 512 + s * 256 + t * 128, 128)
+        return pltpu.make_async_remote_copy(
+            src_ref=ref, dst_ref=ref,
+            send_sem=wy_send.at[mat, k, s, t], recv_sem=wy_recv.at[mat, others[k], s, t],
+            device_id={"band": (ahead, behind)[t], "mp": m}, device_id_type=MESH,
+        )
+
+    def weight_relay(k, s):
+        for mat in range(2):
+            ref = weight_part(others[k], mat, parity * 512 + s * 256, 256)
+            pltpu.make_async_remote_copy(
+                src_ref=ref, dst_ref=ref,
+                send_sem=wx_send.at[mat, k, s], recv_sem=wx_recv.at[mat, others[k], s],
+                device_id={"mp": 2 * others[k] + c}, device_id_type=MESH,
+            ).wait_recv()
+            for t in range(2):
+                weight_y(mat, k, s, t, parity).start()
+
+    def weight_wait(k):
+        for mat in range(2):
+            for s in range(2):
+                for t in range(2):
+                    weight_y(mat, k, s, t, 1 - parity).wait_recv()
+
+    spread_o = Spread(wo, wo_all, layers, z, band_in_z, x, c, m, (o0, o1, o2, o3, o4))
+    spread_p = Spread(pwo, pwo_all, ring, y, band_in_y, x, c, m, (p0, p1, p2, p3, p4))
+
+    def head_piece(cc, xx):
+        return heads.at[
+            pl.ds(pl.multiple_of(xx * OWN, OWN), OWN), pl.ds(pl.multiple_of(cc * 512, 512), 512)
         ]
 
-    ring_o = Ring(eighth(wo_all), lambda half: wo.at[pl.ds(half * HALF, HALF), :], os, orr).bind(x, c)
-    ring_p = Ring(eighth(pwo_all), lambda half: pwo.at[pl.ds(half * HALF, HALF), :], ps, pr).bind(x, c)
-
-    def head_piece(cc, xx, half):
-        return heads.at[
-            pl.ds(pl.multiple_of(xx * OWN + half * (OWN // 2), OWN // 2), OWN // 2),
-            pl.ds(pl.multiple_of(cc * 512, 512), 512),
-        ]
-
-    ring_h = Ring(head_piece, lambda half: head_piece(c, x, half), hs, hr).bind(x, c)
-
-    def out_piece(cc, xx, half):
-        return heads2.at[pl.ds(half * 128, 128), at_cols((cc * 4 + xx) * COLS)]
-
-    ring_g = Ring(out_piece, lambda half: out_piece(c, x, half), gs, gr).bind(x, c)
-
-    ring_k.start()
-    ring_v.start()
+    def out_piece(cc, xx):
+        return heads2.at[:, at_cols((cc * 4 + xx) * COLS)]
+
+    ring_h = Ring(head_piece, hs, hr, x, c)
+    ring_g = Ring(out_piece, gs, gr, x, c)
+
+    for mat in range(2):
+        for k in range(2):
+            weight_x(mat, k, 0).start()
+    spread_o.start()
+    for k, s in ((0, 1), (1, 1), (2, 0), (2, 1)):
+        for mat in range(2):
+            weight_x(mat, k, s).start()
     grid_own = pl.ds(pl.multiple_of(c * ROWS, ROWS), ROWS)
     grid_other = pl.ds(pl.multiple_of((1 - c) * ROWS, ROWS), ROWS)
     to_partner = pltpu.make_async_remote_copy(
@@ -287,12 +369,20 @@
         normed[at, :] = norm_rows(raw[at, :], grid_gain[...]).astype(BF16)
         return carry
 
+    base = b * (8 * ROWS) + x * (2 * ROWS)
+    rim_row = jnp.where(is_top, ROWS, 0)
     local[2].wait()
     lax.fori_loop(c * 8, c * 8 + 8, grid_block, 0)
-
-    base = b * (8 * ROWS) + x * (2 * ROWS)
-    rim_row = jnp.where(is_top, ROWS, 0)
-    fill_bias(edges, counts, bias, base, 2 * ROWS)
+    weight_relay(0, 0)
+    weight_relay(1, 0)
+    sort_edges(edges, counts, columns, base)
+    fill_bias(columns, bias, 2 * ROWS, 0, NODES // 2)
+    spread_o.spread()
+    weight_relay(0, 1)
+    weight_relay(1, 1)
+    spread_p.start()
+    fill_bias(columns, bias, 2 * ROWS, NODES // 2, NODES)
+    weight_relay(2, 0)
     vals[:, COLS:] = jnp.ones((2 * ROWS, COLS), BF16)
     stat[...] = jnp.zeros_like(stat)
     stat_r[...] = jnp.zeros_like(stat_r)
@@ -302,12 +392,16 @@
         device_id={"mp": 2 * x + 1 - c}, device_id_type=MESH,
     ).wait_recv()
     lax.fori_loop((1 - c) * 8, (1 - c) * 8 + 8, grid_block, 0)
+    weight_relay(2, 1)
 
     @pl.when(is_rim)
     def _():
         for one in edge_copies:
             one.wait_recv()
-        fill_bias(edges_r, counts_r, bias_r, base + rim_row, ROWS)
+        sort_edges(edges_r, counts_r, columns, base + rim_row)
+        fill_bias(columns, bias_r, ROWS, 0, NODES)
+
+    spread_p.spread()
 
     def part_copy(xs, d):
         xx = lax.rem(x + d + 1, 4)
@@ -369,19 +463,11 @@
             local[0].wait()
             local[1].wait()
 
-        @pl.when(j == 1)
-        def _():
-            for ring in (ring_k, ring_v):
-                ring.relay_left(False)
-            for ring in (ring_k, ring_v):
-                ring.relay_right(False)
-            ring_o.start()
-            ring_o.start_partner()
-
-        @pl.when(j == 3)
-        def _():
-            for ring in (ring_k, ring_v):
-                ring.relay_far(False)
+        for k in range(3):
+
+            @pl.when(j == k + 1)
+            def _():
+                weight_wait(k)
 
         @pl.when(j > 0)
         def _():
@@ -422,8 +508,6 @@
     st[x] = stat[mine, :]
     for xs in range(4):
         po[x, xs] = part[xs, mine, :]
-    ring_o.relay_left(True)
-    ring_o.relay_right(True)
 
     def arrivals(i):
         for xs in range(4):
@@ -460,25 +544,31 @@
         heads[mine, at_cols(c * 512 + xs * COLS)] = total.astype(BF16)
 
     ring_h.start()
-    ring_h.start_partner()
-    ring_h.relay_left(True)
-    ring_h.relay_right(True)
-    ring_h.relay_far(True)
-    ring_p.start()
-    ring_p.start_partner()
-    ring_o.relay_far(True)
+    ring_h.relay()
     local[3].wait()
-    ring_o.from_partner()
+    spread_o.collect()
+
+    def half_product(left, right, cc, at):
+        return jnp.dot(
+            left[:, pl.ds(pl.multiple_of(cc * 512, 512), 512)],
+            right[pl.ds(cc * 4, 4), :, at].reshape(512, 256),
+            preferred_element_type=F32,
+        )
+
+    def latent_first(n, carry):
+        at = pl.ds(pl.multiple_of(n * 256, 256), 256)
+        latent[:, at] = hidden[:, at].astype(F32) + half_product(heads, wo_all, c, at)
+        return carry
+
+    def latent_second(n, carry):
+        at = pl.ds(pl.multiple_of(n * 256, 256), 256)
+        latent[:, at] = latent[:, at] + half_product(heads, wo_all, 1 - c, at)
+        return carry
+
+    lax.fori_loop(0, 4, latent_first, 0)
     ring_h.from_partner()
-
-    def latent_block(n, carry):
-        at = pl.ds(pl.multiple_of(n * 256, 256), 256)
-        latent[:, at] = hidden[:, at].astype(F32) + jnp.dot(
-            heads[...], wo_all[:, at], preferred_element_type=F32
-        )
-        return carry
-
-    lax.fori_loop(0, 4, latent_block, 0)
+    spread_o.from_partner()
+    lax.fori_loop(0, 4, latent_second, 0)
 
     def latent_norm(i, carry):
         at = pl.ds(pl.multiple_of(i * 64, 64), 64)
@@ -505,8 +595,8 @@
         kv_copy(k).start()
     local[7].wait()
     query = jnp.dot(node[...], pq[...], preferred_element_type=F32).astype(BF16) * BF16(0.125)
-    ring_p.relay_left(True)
-    ring_p.relay_right(True)
+    local[4].wait()
+    spread_p.collect()
     for k in range(2):
         kv_copy(k).wait_recv()
 
@@ -520,28 +610,31 @@
     heads2[:, at_cols(slot * COLS)] = result
 
     ring_g.start()
-    ring_g.start_partner()
-    ring_g.relay_left(True)
-    ring_g.relay_right(True)
-    ring_g.relay_far(True)
-    ring_p.relay_far(True)
-    local[4].wait()
-    ring_p.from_partner()
+    ring_g.relay()
+
+    def mixed_first(n, carry):
+        at = pl.ds(pl.multiple_of(n * 256, 256), 256)
+        latent[:, at] = latent[:, at] + half_product(heads2, pwo_all, c, at)
+        return carry
+
+    def mixed_second(n, carry):
+        at = pl.ds(pl.multiple_of(n * 256, 256), 256)
+        out[:, at] = (latent[:, at] + half_product(heads2, pwo_all, 1 - c, at)).astype(BF16)
+        return carry
+
+    lax.fori_loop(0, 4, mixed_first, 0)
     ring_g.from_partner()
-
-    def mixed_block(n, carry):
-        at = pl.ds(pl.multiple_of(n * 256, 256), 256)
-        out[:, at] = (
-            latent[:, at] + jnp.dot(heads2[...], pwo_all[:, at], preferred_element_type=F32)
-        ).astype(BF16)
-        return carry
-
-    lax.fori_loop(0, 4, mixed_block, 0)
-
-    for ring in (ring_k, ring_v):
-        ring.drain(False)
-    for ring in (ring_o, ring_p, ring_h, ring_g):
-        ring.drain(True)
+    spread_p.from_partner()
+    lax.fori_loop(0, 4, mixed_second, 0)
+
+    for mat in range(2):
+        for k in range(3):
+            for s in range(2):
+                weight_x(mat, k, s).wait_send()
+                for t in range(2):
+                    weight_y(mat, k, s, t, parity).wait_send()
+    for one in (spread_o, spread_p, ring_h, ring_g):
+        one.drain()
     to_partner.wait_send()
     for d in range(3):
         q_copy(d).wait_send()
@@ -564,18 +657,22 @@
 
 def solution(mesh):
     bands = mesh.shape["band"]
+    ring = RING if bands % RING == 0 else 2
+    layers = bands // ring
 
     def step(
         grid_latent, grid_gain, hidden_in, hid_gain, enc_wq, enc_wk, enc_wv, enc_wo,
         enc_edges, enc_counts, proc_gain, proc_wq, proc_wk, proc_wv, proc_wo,
     ):
         counts = enc_counts.reshape(1, NODES)
+        edges = enc_edges.T
         hbm = pl.BlockSpec(memory_space=pl.ANY)
         vmem = pl.BlockSpec(memory_space=pltpu.VMEM)
         dma = pltpu.SemaphoreType.DMA
-        ring_sems = [dma((3, 4, 2)), dma((2, 4, 2))]
+        spread_sems = lambda n: [dma((3,)), dma((4,)), dma((3, n)), dma((4, n)), dma((2,))]
+        ring_sems = [dma((7,)), dma((2, 4))]
         return pl.pallas_call(
-            functools.partial(kernel, bands),
+            functools.partial(kernel, bands, ring),
             out_shape=jax.ShapeDtypeStruct((NODES, D), BF16),
             in_specs=[hbm] * 10 + [vmem] * 7,
             out_specs=vmem,
@@ -590,8 +687,9 @@
                 pltpu.VMEM((2 * ROWS, 2 * COLS), BF16),
                 pltpu.VMEM((NODES, 2 * ROWS), F32),
                 pltpu.VMEM((NODES, ROWS), F32),
-                pltpu.VMEM((NODES, SLOTS), jnp.int32),
+                pltpu.VMEM((SLOTS, NODES), jnp.int32),
                 pltpu.VMEM((1, NODES), jnp.int32),
+                pltpu.VMEM((NODES, COLS), F32),
                 pltpu.VMEM((4, NODES, COLS), BF16),
                 pltpu.VMEM((NODES, 128), F32),
                 pltpu.VMEM((4, NODES, COLS), BF16),
@@ -599,15 +697,18 @@
                 pltpu.VMEM((6, 4, OWN, COLS), BF16),
                 pltpu.VMEM((6, OWN, 128), F32),
                 pltpu.VMEM((NODES, D), BF16),
-                pltpu.VMEM((D, D), BF16),
-                pltpu.VMEM((D, D), BF16),
+                pltpu.VMEM((8, COLS, D), BF16),
+                pltpu.VMEM((8, COLS, D), BF16),
                 pltpu.VMEM((NODES, D), F32),
                 pltpu.VMEM((D, 2 * COLS), BF16),
                 pltpu.VMEM((D, COLS), BF16),
                 pltpu.VMEM((NODES + 2 * WIN, 2 * COLS), BF16),
                 pltpu.VMEM((NODES, D), BF16),
             ]
-            + ring_sems * 6
+            + [dma((2, 3, 2)), dma((2, 4, 2)), dma((2, 3, 2, 2)), dma((2, 4, 2, 2))]
+            + spread_sems(layers)
+            + spread_sems(ring)
+            + ring_sems * 2
             + [
                 dma((8,)),
                 dma((2,)),
@@ -623,8 +724,8 @@
                 collective_id=0, has_side_effects=True, vmem_limit_bytes=60 * 1024 * 1024
             ),
         )(
-            grid_latent, enc_wk, enc_wv, enc_wo, proc_wk, proc_wv, proc_wq, proc_wo, enc_edges, counts,
-            grid_gain.reshape(1, D), hidden_in, hid_gain.reshape(1, D), enc_wq, enc_edges, counts,
+            grid_latent, enc_wk, enc_wv, enc_wo, proc_wk, proc_wv, proc_wq, proc_wo, edges, counts,
+            grid_gain.reshape(1, D), hidden_in, hid_gain.reshape(1, D), enc_wq, edges, counts,
             proc_gain.reshape(1, D),
         )
 

time: 91.5 us -> 95.2 us (1.040)
  Pallas kernels: 87.9 us -> 93.1 us
  local copies, waits for them, and re-layouts: 3.38 us -> 1.87 us
    pallas_call x1, Pallas kernels: 87.9 us -> 93.1 us  [step(): pl.pallas_call(functools.partial(kernel, bands, ring), out_shape=jax.Shap...]
    unnamed x2 -> x1, local copies, waits for them, and re-layouts: 3.38 us -> 1.87 us
where the time goes in v2:
time: 95.2 us; the launch traced here: 95 us
  Pallas kernels  93.1 us (98%)
  local copies, waits for them, and re-layouts  1.87 us (2%)
    pallas_call x1, Pallas kernels, step(): pl.pallas_call(functools.partial(kernel, bands, ring), out_shape=jax.Shap...  93.1 us

profile of v2, /device:TPU:1, one launch (start us, length us, event | category | flops | bytes accessed | tf_op | source)
XLA Modules:
  0.0 95.0 jit_solution(17673862676233812453)
XLA Ops:
  0.0 93.1 %shard_map.145 = bf16[256,1024]{1,0:T(8,128)(2,1)} custom-call(bf16[512,1024]{1,0:T(8,128)(2,1)} %grid.1, bf16[1024,128]{1,0:T(8,128)(2,1)} %wk.1, bf16[1024,128]{1,0:T(8,128)(2,1)} %wv.1, bf16[128,1024]{1,0:T(8,128)(2,1)} %wo.1, bf16[1024,128]{1,0:T(8,128)(2,1)} %pwk.1, bf16[1024,128]{1,0:T(8,128)(2,1)} %pwv.1, bf16[1024,128]{1,0:T(8,128)(2,1)} %pwq.1, ...), custom_call_target="tpu_custom_call" | custom-call | tf_op jit(solution)/shard_map/pallas_call | solution.py:674
  93.2 1.9 %copy.17 = bf16[256,1024]{1,0:T(8,128)(2,1)} copy(bf16[256,1024]{1,0:T(8,128)(2,1)} %shard_map.145) | data formatting | bytes 1048576

commit v3 on v2

--- a/solution.py
+++ b/solution.py
@@ -148,22 +148,30 @@
         self.to_partner(self.c).wait_send()
 
 
-def sort_edges(edges_ref, counts_ref, columns_ref, base):
+def code_of(index):
+    high = jnp.clip(index >> 7, 0, 7)
+    return ((COLS + (index & 127)) << high).astype(F32)
+
+
+def sort_edges(edges_ref, counts_ref, columns_ref, base, width):
     slot = lax.broadcasted_iota(jnp.int32, (SLOTS, NODES), 0)
-    live = jnp.where(slot < counts_ref[...], edges_ref[...] - base, -1).astype(F32)
-    columns_ref[...] = jnp.concatenate([live, jnp.full((COLS - SLOTS, NODES), -1.0, F32)], axis=0).T
+    index = edges_ref[...] - base
+    live = (slot < counts_ref[...]) & (index >= 0) & (index < width)
+    codes = jnp.where(live, code_of(index), -1.0)
+    columns_ref[...] = jnp.concatenate([codes, jnp.full((COLS - SLOTS, NODES), -1.0, F32)], axis=0).T.astype(BF16)
 
 
 def fill_bias(columns_ref, bias_ref, width, begin, end):
     step = 16
-    column = lax.broadcasted_iota(jnp.int32, (step, width), 1).astype(F32)
+    column = code_of(lax.broadcasted_iota(jnp.int32, (step, width), 1)).astype(BF16)
 
     def block(i, carry):
         at = pl.multiple_of(i * step, step)
         edges = columns_ref[pl.ds(at, step), :]
-        total = jnp.zeros((step, width), F32)
+        total = jnp.zeros((step, width), BF16)
         for s in range(SLOTS):
-            total = total + jnp.where(edges[:, s : s + 1] == column, 1.0, 0.0)
+            total = total + jnp.where(edges[:, s : s + 1] == column, BF16(1), BF16(0))
+        total = total.astype(F32)
         bias_ref[pl.ds(at, step), :] = jnp.where(
             total > 0.0, jnp.log(jnp.maximum(total, 1.0)), NEG
         )
@@ -193,7 +201,7 @@
     grid_gain, hidden, hid_gain, wq, edges, counts, proc_gain,
     out,
     raw, normed, node, w, q, qr, keys, vals, bias, bias_r, edges_r, counts_r, columns,
-    part, stat, part_r, stat_r, po, st, heads, wo_all, pwo_all, latent, pw, pq, kvp, heads2,
+    part, stat, stat_t, part_r, stat_r, stat_rt, spare, po, st, heads, wo_all, pwo_all, latent, pw, pq, kvp, heads2,
     wx_send, wx_recv, wy_send, wy_recv,
     o0, o1, o2, o3, o4, p0, p1, p2, p3, p4, hs, hr, gs, gr,
     loc, grid_sem, edge_sem, q_send, q_recv, qr_send, qr_recv,
@@ -236,7 +244,7 @@
     local = [
         pltpu.make_async_copy(wk, w.at[x, :, 0:COLS], loc.at[0]),
         pltpu.make_async_copy(wv, w.at[x, :, COLS:], loc.at[1]),
-        pltpu.make_async_copy(grid, raw.at[pl.ds(pl.multiple_of(c * ROWS, ROWS), ROWS), :], loc.at[2]),
+        pltpu.make_async_copy(grid, raw, loc.at[2]),
         pltpu.make_async_copy(wo, wo_all.at[slot], loc.at[3]),
         pltpu.make_async_copy(pwo, pwo_all.at[slot], loc.at[4]),
         pltpu.make_async_copy(pwk, pw.at[:, 0:COLS], loc.at[5]),
@@ -287,7 +295,7 @@
                     weight_y(mat, k, s, t, 1 - parity).wait_recv()
 
     spread_o = Spread(wo, wo_all, layers, z, band_in_z, x, c, m, (o0, o1, o2, o3, o4))
-    spread_p = Spread(pwo, pwo_all, ring, y, band_in_y, x, c, m, (p0, p1, p2, p3, p4))
+    spread_p = Spread(pwo, pwo_all, layers, z, band_in_z, x, c, m, (p0, p1, p2, p3, p4))
 
     def head_piece(cc, xx):
         return heads.at[
@@ -304,16 +312,17 @@
         for k in range(2):
             weight_x(mat, k, 0).start()
     spread_o.start()
-    for k, s in ((0, 1), (1, 1), (2, 0), (2, 1)):
-        for mat in range(2):
-            weight_x(mat, k, s).start()
+    for mat in range(2):
+        for k in range(2):
+            weight_x(mat, k, 1).start()
     grid_own = pl.ds(pl.multiple_of(c * ROWS, ROWS), ROWS)
     grid_other = pl.ds(pl.multiple_of((1 - c) * ROWS, ROWS), ROWS)
-    to_partner = pltpu.make_async_remote_copy(
-        src_ref=grid, dst_ref=raw.at[grid_own, :], send_sem=grid_sem.at[0], recv_sem=grid_sem.at[1],
-        device_id={"mp": 2 * x + 1 - c}, device_id_type=MESH,
-    )
-    to_partner.start()
+
+    def rows_to_partner(at):
+        return pltpu.make_async_remote_copy(
+            src_ref=normed.at[at, :], dst_ref=normed.at[at, :], send_sem=grid_sem.at[0], recv_sem=grid_sem.at[1],
+            device_id={"mp": 2 * x + 1 - c}, device_id_type=MESH,
+        )
 
     def rim_input(source, target, k, band):
         return pltpu.make_async_remote_copy(
@@ -363,45 +372,41 @@
         q_copy(d).start()
     for k in range(2):
         qr_copy(k).start()
+    for mat in range(2):
+        for s in range(2):
+            weight_x(mat, 2, s).start()
+    spread_p.start()
 
     def grid_block(i, carry):
         at = pl.ds(pl.multiple_of(i * 64, 64), 64)
-        normed[at, :] = norm_rows(raw[at, :], grid_gain[...]).astype(BF16)
+        normed[pl.ds(pl.multiple_of(c * ROWS + i * 64, 64), 64), :] = norm_rows(raw[at, :], grid_gain[...]).astype(BF16)
         return carry
 
     base = b * (8 * ROWS) + x * (2 * ROWS)
     rim_row = jnp.where(is_top, ROWS, 0)
     local[2].wait()
-    lax.fori_loop(c * 8, c * 8 + 8, grid_block, 0)
+    lax.fori_loop(0, ROWS // 64, grid_block, 0)
+    rows_to_partner(grid_own).start()
+    sort_edges(edges, counts, columns, base, 2 * ROWS)
+    fill_bias(columns, bias, 2 * ROWS, 0, NODES // 2)
     weight_relay(0, 0)
     weight_relay(1, 0)
-    sort_edges(edges, counts, columns, base)
-    fill_bias(columns, bias, 2 * ROWS, 0, NODES // 2)
+    fill_bias(columns, bias, 2 * ROWS, NODES // 2, NODES)
     spread_o.spread()
     weight_relay(0, 1)
     weight_relay(1, 1)
-    spread_p.start()
-    fill_bias(columns, bias, 2 * ROWS, NODES // 2, NODES)
-    weight_relay(2, 0)
     vals[:, COLS:] = jnp.ones((2 * ROWS, COLS), BF16)
     stat[...] = jnp.zeros_like(stat)
     stat_r[...] = jnp.zeros_like(stat_r)
-
-    pltpu.make_async_remote_copy(
-        src_ref=grid, dst_ref=raw.at[grid_other, :], send_sem=grid_sem.at[0], recv_sem=grid_sem.at[1],
-        device_id={"mp": 2 * x + 1 - c}, device_id_type=MESH,
-    ).wait_recv()
-    lax.fori_loop((1 - c) * 8, (1 - c) * 8 + 8, grid_block, 0)
-    weight_relay(2, 1)
 
     @pl.when(is_rim)
     def _():
         for one in edge_copies:
             one.wait_recv()
-        sort_edges(edges_r, counts_r, columns, base + rim_row)
+        sort_edges(edges_r, counts_r, columns, base + rim_row, ROWS)
         fill_bias(columns, bias_r, ROWS, 0, NODES)
 
-    spread_p.spread()
+    rows_to_partner(grid_other).wait_recv()
 
     def part_copy(xs, d):
         xx = lax.rem(x + d + 1, 4)
@@ -425,16 +430,14 @@
     def stat_copy(d):
         xx = lax.rem(x + d + 1, 4)
         return pltpu.make_async_remote_copy(
-            src_ref=stat.at[pl.ds(pl.multiple_of(xx * OWN, OWN), OWN), :],
-            dst_ref=st.at[x],
+            src_ref=stat_t.at[lax.div(xx, 2)], dst_ref=st.at[x],
             send_sem=st_send.at[d], recv_sem=st_recv.at[x],
             device_id={"mp": 2 * xx + c}, device_id_type=MESH,
         )
 
     def rim_stat_copy(xx):
         return pltpu.make_async_remote_copy(
-            src_ref=stat_r.at[pl.ds(xx * OWN, OWN), :],
-            dst_ref=st.at[rim_slot],
+            src_ref=stat_rt.at[xx // 2], dst_ref=st.at[rim_slot],
             send_sem=rs_send.at[xx], recv_sem=st_recv.at[rim_slot],
             device_id={"band": rim_to, "mp": 2 * xx + c}, device_id_type=MESH,
         )
@@ -455,24 +458,7 @@
 
         lax.fori_loop(0, NODES // chunk, block, 0)
 
-    def head_step(j, carry):
-        xs = lax.rem(x + jnp.where(j == 0, 0, jnp.where(j == 1, 3, jnp.where(j == 2, 1, 2))), 4)
-
-        @pl.when(j == 0)
-        def _():
-            local[0].wait()
-            local[1].wait()
-
-        for k in range(3):
-
-            @pl.when(j == k + 1)
-            def _():
-                weight_wait(k)
-
-        @pl.when(j > 0)
-        def _():
-            q_arrival(q, q_recv, xs).wait_recv()
-
+    def slice_of(xs):
         def project(i, inner):
             at = pl.ds(pl.multiple_of(i * ROWS, ROWS), ROWS)
             both = jnp.dot(normed[at, :], w[xs], preferred_element_type=F32).astype(BF16)
@@ -492,20 +478,41 @@
         attend(xs, q, bias, part, stat, 0, 2 * ROWS)
         for d in range(3):
             part_copy(xs, d).start()
-        return carry
-
-    lax.fori_loop(0, 4, head_step, 0)
-
+
+    def head_step(j, carry):
+        xs = lax.rem(x + jnp.where(j == 1, 3, jnp.where(j == 2, 1, 2)), 4)
+        for k in range(3):
+
+            @pl.when(j == k + 1)
+            def _():
+                weight_wait(k)
+
+        q_arrival(q, q_recv, xs).wait_recv()
+        slice_of(xs)
+        return carry
+
+    local[0].wait()
+    local[1].wait()
+    slice_of(x)
+    weight_relay(2, 0)
+    weight_relay(2, 1)
+    spread_p.spread()
+    lax.fori_loop(1, 4, head_step, 0)
+
+    for half in range(2):
+        stat_t[half] = stat[half * 128 : half * 128 + 128, :].T[0:8]
     for d in range(3):
         stat_copy(d).start()
 
     @pl.when(is_rim)
     def _():
+        for half in range(2):
+            stat_rt[half] = stat_r[half * 128 : half * 128 + 128, :].T[0:8]
         for xx in range(4):
             rim_stat_copy(xx).start()
 
     mine = pl.ds(pl.multiple_of(x * OWN, OWN), OWN)
-    st[x] = stat[mine, :]
+    st[x] = stat_t[lax.div(x, 2)]
     for xs in range(4):
         po[x, xs] = part[xs, mine, :]
 
@@ -534,12 +541,15 @@
     for i in range(1, 6):
         whole = whole + shares[i]
     shares = [one / whole for one in shares]
+    spare[...] = jnp.concatenate(shares + [jnp.zeros((128 - 48, 128), F32)], axis=0).T
+    share = spare[pl.ds(pl.multiple_of(lax.rem(x, 2) * OWN, OWN), OWN), :]
     first = lax.broadcasted_iota(jnp.int32, (OWN, COLS), 1) < HALF
     for xs in range(4):
         total = jnp.zeros((OWN, COLS), F32)
         for i in range(6):
-            left = jnp.broadcast_to(shares[i][:, 2 * xs : 2 * xs + 1], (OWN, COLS))
-            right = jnp.broadcast_to(shares[i][:, 2 * xs + 1 : 2 * xs + 2], (OWN, COLS))
+            at = i * 8 + 2 * xs
+            left = jnp.broadcast_to(share[:, at : at + 1], (OWN, COLS))
+            right = jnp.broadcast_to(share[:, at + 1 : at + 2], (OWN, COLS))
             total = total + jnp.where(first, left, right) * po[i, xs].astype(F32)
         heads[mine, at_cols(c * 512 + xs * COLS)] = total.astype(BF16)
 
@@ -635,7 +645,7 @@
                     weight_y(mat, k, s, t, parity).wait_send()
     for one in (spread_o, spread_p, ring_h, ring_g):
         one.drain()
-    to_partner.wait_send()
+    rows_to_partner(grid_own).wait_send()
     for d in range(3):
         q_copy(d).wait_send()
         stat_copy(d).wait_send()
@@ -677,7 +687,7 @@
             in_specs=[hbm] * 10 + [vmem] * 7,
             out_specs=vmem,
             scratch_shapes=[
-                pltpu.VMEM((2 * ROWS, D), BF16),
+                pltpu.VMEM((ROWS, D), BF16),
                 pltpu.VMEM((2 * ROWS, D), BF16),
                 pltpu.VMEM((NODES, D), BF16),
                 pltpu.VMEM((4, D, 2 * COLS), BF16),
@@ -689,13 +699,16 @@
                 pltpu.VMEM((NODES, ROWS), F32),
                 pltpu.VMEM((SLOTS, NODES), jnp.int32),
                 pltpu.VMEM((1, NODES), jnp.int32),
-                pltpu.VMEM((NODES, COLS), F32),
+                pltpu.VMEM((NODES, COLS), BF16),
                 pltpu.VMEM((4, NODES, COLS), BF16),
                 pltpu.VMEM((NODES, 128), F32),
+                pltpu.VMEM((2, 8, 128), F32),
                 pltpu.VMEM((4, NODES, COLS), BF16),
                 pltpu.VMEM((NODES, 128), F32),
+                pltpu.VMEM((2, 8, 128), F32),
+                pltpu.VMEM((128, 128), F32),
                 pltpu.VMEM((6, 4, OWN, COLS), BF16),
-                pltpu.VMEM((6, OWN, 128), F32),
+                pltpu.VMEM((6, 8, 128), F32),
                 pltpu.VMEM((NODES, D), BF16),
                 pltpu.VMEM((8, COLS, D), BF16),
                 pltpu.VMEM((8, COLS, D), BF16),
@@ -706,8 +719,7 @@
                 pltpu.VMEM((NODES, D), BF16),
             ]
             + [dma((2, 3, 2)), dma((2, 4, 2)), dma((2, 3, 2, 2)), dma((2, 4, 2, 2))]
-            + spread_sems(layers)
-            + spread_sems(ring)
+            + spread_sems(layers) * 2
             + ring_sems * 2
             + [
                 dma((8,)),

time: 95.2 us -> 88.8 us (0.933)
  Pallas kernels: 93.1 us -> 86.7 us
    pallas_call x1, Pallas kernels: 93.1 us -> 86.7 us  [step(): pl.pallas_call(functools.partial(kernel, bands, ring), out_shape=jax.Shap...]
where the time goes in v3:
time: 88.8 us; the launch traced here: 88.6 us
  Pallas kernels  86.7 us (98%)
  local copies, waits for them, and re-layouts  1.87 us (2%)
    pallas_call x1, Pallas kernels, step(): pl.pallas_call(functools.partial(kernel, bands, ring), out_shape=jax.Shap...  86.7 us
    unnamed x1, local copies, waits for them, and re-layouts  1.87 us

profile of v3, /device:TPU:1, one launch (start us, length us, event | category | flops | bytes accessed | tf_op | source)
XLA Modules:
  0.0 88.6 jit_solution(1183085067644274385)
XLA Ops:
  0.0 86.7 %shard_map.145 = bf16[256,1024]{1,0:T(8,128)(2,1)} custom-call(bf16[512,1024]{1,0:T(8,128)(2,1)} %grid.1, bf16[1024,128]{1,0:T(8,128)(2,1)} %wk.1, bf16[1024,128]{1,0:T(8,128)(2,1)} %wv.1, bf16[128,1024]{1,0:T(8,128)(2,1)} %wo.1, bf16[1024,128]{1,0:T(8,128)(2,1)} %pwk.1, bf16[1024,128]{1,0:T(8,128)(2,1)} %pwv.1, bf16[1024,128]{1,0:T(8,128)(2,1)} %pwq.1, ...), custom_call_target="tpu_custom_call" | custom-call | tf_op jit(solution)/shard_map/pallas_call | solution.py:684
  86.7 1.9 %copy.17 = bf16[256,1024]{1,0:T(8,128)(2,1)} copy(bf16[256,1024]{1,0:T(8,128)(2,1)} %shard_map.145) | data formatting | bytes 1048576

commit v4 on v3

--- a/solution.py
+++ b/solution.py
@@ -158,26 +158,31 @@
     index = edges_ref[...] - base
     live = (slot < counts_ref[...]) & (index >= 0) & (index < width)
     codes = jnp.where(live, code_of(index), -1.0)
-    columns_ref[...] = jnp.concatenate([codes, jnp.full((COLS - SLOTS, NODES), -1.0, F32)], axis=0).T.astype(BF16)
-
-
-def fill_bias(columns_ref, bias_ref, width, begin, end):
+    columns_ref[...] = jnp.concatenate([codes, jnp.full((COLS - SLOTS, NODES), -1.0, F32)], axis=0).T
+
+
+def fill_bias(columns_ref, bias_ref, width):
     step = 16
-    column = code_of(lax.broadcasted_iota(jnp.int32, (step, width), 1)).astype(BF16)
+    lane = lax.broadcasted_iota(jnp.int32, (step, COLS), 1)
+    columns = [code_of(lane + k * COLS).astype(BF16) for k in range(width // COLS)]
 
     def block(i, carry):
-        at = pl.multiple_of(i * step, step)
-        edges = columns_ref[pl.ds(at, step), :]
-        total = jnp.zeros((step, width), BF16)
+        at = pl.ds(pl.multiple_of(i * step, step), step)
+        edges = columns_ref[at, :]
+        totals = [jnp.zeros((step, COLS), BF16) for _ in columns]
         for s in range(SLOTS):
-            total = total + jnp.where(edges[:, s : s + 1] == column, BF16(1), BF16(0))
-        total = total.astype(F32)
-        bias_ref[pl.ds(at, step), :] = jnp.where(
-            total > 0.0, jnp.log(jnp.maximum(total, 1.0)), NEG
-        )
-        return carry
-
-    lax.fori_loop(begin // step, end // step, block, 0)
+            edge = jnp.broadcast_to(edges[:, s : s + 1], (step, COLS)).astype(BF16)
+            totals = [
+                total + jnp.where(edge == column, BF16(1), BF16(0)) for total, column in zip(totals, columns)
+            ]
+        for k, total in enumerate(totals):
+            total = total.astype(F32)
+            bias_ref[at, k * COLS : (k + 1) * COLS] = jnp.where(
+                total > 0.0, jnp.log(jnp.maximum(total, 1.0)), NEG
+            )
+        return carry
+
+    lax.fori_loop(0, NODES // step, block, 0)
 
 
 def two_heads(query, keys, values, bias):
@@ -388,13 +393,10 @@
     lax.fori_loop(0, ROWS // 64, grid_block, 0)
     rows_to_partner(grid_own).start()
     sort_edges(edges, counts, columns, base, 2 * ROWS)
-    fill_bias(columns, bias, 2 * ROWS, 0, NODES // 2)
+    fill_bias(columns, bias, 2 * ROWS)
     weight_relay(0, 0)
     weight_relay(1, 0)
-    fill_bias(columns, bias, 2 * ROWS, NODES // 2, NODES)
     spread_o.spread()
-    weight_relay(0, 1)
-    weight_relay(1, 1)
     vals[:, COLS:] = jnp.ones((2 * ROWS, COLS), BF16)
     stat[...] = jnp.zeros_like(stat)
     stat_r[...] = jnp.zeros_like(stat_r)
@@ -404,7 +406,7 @@
         for one in edge_copies:
             one.wait_recv()
         sort_edges(edges_r, counts_r, columns, base + rim_row, ROWS)
-        fill_bias(columns, bias_r, ROWS, 0, NODES)
+        fill_bias(columns, bias_r, ROWS)
 
     rows_to_partner(grid_other).wait_recv()
 
@@ -456,7 +458,7 @@
             stat_ref[at, :] = jnp.where(lane == 2 * xs + 1, sums[1], old)
             return carry
 
-        lax.fori_loop(0, NODES // chunk, block, 0)
+        lax.fori_loop(0, NODES // chunk, block, 0, unroll=True)
 
     def slice_of(xs):
         def project(i, inner):
@@ -487,6 +489,11 @@
             def _():
                 weight_wait(k)
 
+        @pl.when(j == 2)
+        def _():
+            weight_relay(2, 0)
+            weight_relay(2, 1)
+
         q_arrival(q, q_recv, xs).wait_recv()
         slice_of(xs)
         return carry
@@ -494,9 +501,8 @@
     local[0].wait()
     local[1].wait()
     slice_of(x)
-    weight_relay(2, 0)
-    weight_relay(2, 1)
-    spread_p.spread()
+    weight_relay(0, 1)
+    weight_relay(1, 1)
     lax.fori_loop(1, 4, head_step, 0)
 
     for half in range(2):
@@ -511,6 +517,7 @@
         for xx in range(4):
             rim_stat_copy(xx).start()
 
+    spread_p.spread()
     mine = pl.ds(pl.multiple_of(x * OWN, OWN), OWN)
     st[x] = stat_t[lax.div(x, 2)]
     for xs in range(4):
@@ -575,10 +582,10 @@
         latent[:, at] = latent[:, at] + half_product(heads, wo_all, 1 - c, at)
         return carry
 
-    lax.fori_loop(0, 4, latent_first, 0)
+    lax.fori_loop(0, 4, latent_first, 0, unroll=True)
     ring_h.from_partner()
     spread_o.from_partner()
-    lax.fori_loop(0, 4, latent_second, 0)
+    lax.fori_loop(0, 4, latent_second, 0, unroll=True)
 
     def latent_norm(i, carry):
         at = pl.ds(pl.multiple_of(i * 64, 64), 64)
@@ -620,30 +627,13 @@
     heads2[:, at_cols(slot * COLS)] = result
 
     ring_g.start()
-    ring_g.relay()
-
-    def mixed_first(n, carry):
-        at = pl.ds(pl.multiple_of(n * 256, 256), 256)
-        latent[:, at] = latent[:, at] + half_product(heads2, pwo_all, c, at)
-        return carry
-
-    def mixed_second(n, carry):
-        at = pl.ds(pl.multiple_of(n * 256, 256), 256)
-        out[:, at] = (latent[:, at] + half_product(heads2, pwo_all, 1 - c, at)).astype(BF16)
-        return carry
-
-    lax.fori_loop(0, 4, mixed_first, 0)
-    ring_g.from_partner()
-    spread_p.from_partner()
-    lax.fori_loop(0, 4, mixed_second, 0)
-
     for mat in range(2):
         for k in range(3):
             for s in range(2):
                 weight_x(mat, k, s).wait_send()
                 for t in range(2):
                     weight_y(mat, k, s, t, parity).wait_send()
-    for one in (spread_o, spread_p, ring_h, ring_g):
+    for one in (spread_o, spread_p, ring_h):
         one.drain()
     rows_to_partner(grid_own).wait_send()
     for d in range(3):
@@ -663,6 +653,25 @@
             rim_stat_copy(xx).wait_send()
             for xs in range(4):
                 rim_copy(xs, xx).wait_send()
+
+    ring_g.relay()
+
+    def mixed_first(n, carry):
+        at = pl.ds(pl.multiple_of(n * 256, 256), 256)
+        latent[:, at] = latent[:, at] + half_product(heads2, pwo_all, c, at)
+        return carry
+
+    def mixed_second(n, carry):
+        at = pl.ds(pl.multiple_of(n * 256, 256), 256)
+        out[:, at] = (latent[:, at] + half_product(heads2, pwo_all, 1 - c, at)).astype(BF16)
+        return carry
+
+    lax.fori_loop(0, 4, mixed_first, 0, unroll=True)
+    ring_g.from_partner()
+    spread_p.from_partner()
+    lax.fori_loop(0, 4, mixed_second, 0, unroll=True)
+
+    ring_g.drain()
 
 
 def solution(mesh):
@@ -699,7 +708,7 @@
                 pltpu.VMEM((NODES, ROWS), F32),
                 pltpu.VMEM((SLOTS, NODES), jnp.int32),
                 pltpu.VMEM((1, NODES), jnp.int32),
-                pltpu.VMEM((NODES, COLS), BF16),
+                pltpu.VMEM((NODES, COLS), F32),
                 pltpu.VMEM((4, NODES, COLS), BF16),
                 pltpu.VMEM((NODES, 128), F32),
                 pltpu.VMEM((2, 8, 128), F32),

time: 88.8 us -> 83.6 us (0.941)
  Pallas kernels: 86.7 us -> 81.5 us
    pallas_call x1, Pallas kernels: 86.7 us -> 81.5 us  [step(): pl.pallas_call(functools.partial(kernel, bands, ring), out_shape=jax.Shap...]
where the time goes in v4:
time: 83.6 us; the launch traced here: 83.4 us
  Pallas kernels  81.5 us (97%)
  local copies, waits for them, and re-layouts  1.87 us (2%)
    pallas_call x1, Pallas kernels, step(): pl.pallas_call(functools.partial(kernel, bands, ring), out_shape=jax.Shap...  81.5 us
    unnamed x1, local copies, waits for them, and re-layouts  1.87 us

profile of v4, /device:TPU:1, one launch (start us, length us, event | category | flops | bytes accessed | tf_op | source)
XLA Modules:
  0.0 83.4 jit_solution(17540658727703456009)
XLA Ops:
  0.0 81.5 %shard_map.145 = bf16[256,1024]{1,0:T(8,128)(2,1)} custom-call(bf16[512,1024]{1,0:T(8,128)(2,1)} %grid.1, bf16[1024,128]{1,0:T(8,128)(2,1)} %wk.1, bf16[1024,128]{1,0:T(8,128)(2,1)} %wv.1, bf16[128,1024]{1,0:T(8,128)(2,1)} %wo.1, bf16[1024,128]{1,0:T(8,128)(2,1)} %pwk.1, bf16[1024,128]{1,0:T(8,128)(2,1)} %pwv.1, bf16[1024,128]{1,0:T(8,128)(2,1)} %pwq.1, ...), custom_call_target="tpu_custom_call" | custom-call | tf_op jit(solution)/shard_map/pallas_call | solution.py:693
  81.6 1.9 %copy.17 = bf16[256,1024]{1,0:T(8,128)(2,1)} copy(bf16[256,1024]{1,0:T(8,128)(2,1)} %shard_map.145) | data formatting | bytes 1048576

commit v5 on v4

--- a/solution.py
+++ b/solution.py
@@ -209,7 +209,7 @@
     part, stat, stat_t, part_r, stat_r, stat_rt, spare, po, st, heads, wo_all, pwo_all, latent, pw, pq, kvp, heads2,
     wx_send, wx_recv, wy_send, wy_recv,
     o0, o1, o2, o3, o4, p0, p1, p2, p3, p4, hs, hr, gs, gr,
-    loc, grid_sem, edge_sem, q_send, q_recv, qr_send, qr_recv,
+    loc, grid_sem, edge_sem, q_send, q_recv, qr_send, qr_recv, out_sem,
     po_send, po_recv, st_send, st_recv, ro_send, rs_send, kv_send, kv_recv,
 ):
     b, m = lax.axis_index("band"), lax.axis_index("mp")
@@ -258,7 +258,23 @@
     ]
     for one in local:
         one.start()
+    def node_block(i, carry):
+        at = pl.ds(pl.multiple_of(i * 64, 64), 64)
+        node[at, :] = norm_rows(hidden[at, :], hid_gain[...]).astype(BF16)
+        return carry
+
+    lax.fori_loop(0, NODES // 64, node_block, 0)
+    q[x] = jnp.dot(node[...], wq[...], preferred_element_type=F32).astype(BF16) * BF16(0.125)
+
+    def grid_block(i, carry):
+        at = pl.ds(pl.multiple_of(i * 64, 64), 64)
+        normed[pl.ds(pl.multiple_of(c * ROWS + i * 64, 64), 64), :] = norm_rows(raw[at, :], grid_gain[...]).astype(BF16)
+        return carry
+
+    local[2].wait()
+    lax.fori_loop(0, ROWS // 64, grid_block, 0)
     pl.semaphore_wait(barrier, 13 + ring + layers)
+
 
     others = [lax.rem(x + d, 4) for d in (3, 1, 2)]
 
@@ -313,13 +329,6 @@
     ring_h = Ring(head_piece, hs, hr, x, c)
     ring_g = Ring(out_piece, gs, gr, x, c)
 
-    for mat in range(2):
-        for k in range(2):
-            weight_x(mat, k, 0).start()
-    spread_o.start()
-    for mat in range(2):
-        for k in range(2):
-            weight_x(mat, k, 1).start()
     grid_own = pl.ds(pl.multiple_of(c * ROWS, ROWS), ROWS)
     grid_other = pl.ds(pl.multiple_of((1 - c) * ROWS, ROWS), ROWS)
 
@@ -347,24 +356,18 @@
         for one in edge_copies:
             one.start()
 
-    def node_block(i, carry):
-        at = pl.ds(pl.multiple_of(i * 64, 64), 64)
-        node[at, :] = norm_rows(hidden[at, :], hid_gain[...]).astype(BF16)
-        return carry
-
-    lax.fori_loop(0, NODES // 64, node_block, 0)
-    q[x] = jnp.dot(node[...], wq[...], preferred_element_type=F32).astype(BF16) * BF16(0.125)
-
     def q_copy(d):
         return pltpu.make_async_remote_copy(
             src_ref=q.at[x], dst_ref=q.at[x], send_sem=q_send.at[d], recv_sem=q_recv.at[x],
             device_id={"mp": 2 * lax.rem(x + d + 1, 4) + c}, device_id_type=MESH,
         )
 
-    def qr_copy(k):
-        return pltpu.make_async_remote_copy(
-            src_ref=q.at[x], dst_ref=qr.at[x], send_sem=qr_send.at[k], recv_sem=qr_recv.at[x],
-            device_id={"band": (down, up)[k], "mp": (6, 0)[k] + c}, device_id_type=MESH,
+    outer = jnp.where(is_top, down, up)
+
+    def qr_copy(xx):
+        return pltpu.make_async_remote_copy(
+            src_ref=q.at[xx], dst_ref=qr.at[xx], send_sem=qr_send.at[xx], recv_sem=qr_recv.at[xx],
+            device_id={"band": outer, "mp": m}, device_id_type=MESH,
         )
 
     def q_arrival(ref, sems, xx):
@@ -373,30 +376,32 @@
             device_id={"mp": 2 * xx + c}, device_id_type=MESH,
         )
 
+    for mat in range(2):
+        for k in range(2):
+            weight_x(mat, k, 0).start()
+    rows_to_partner(grid_own).start()
     for d in range(3):
         q_copy(d).start()
-    for k in range(2):
-        qr_copy(k).start()
+
+    @pl.when(is_rim)
+    def _():
+        qr_copy(x).start()
+
+    spread_o.start()
+    for mat in range(2):
+        for k in range(2):
+            weight_x(mat, k, 1).start()
     for mat in range(2):
         for s in range(2):
             weight_x(mat, 2, s).start()
     spread_p.start()
 
-    def grid_block(i, carry):
-        at = pl.ds(pl.multiple_of(i * 64, 64), 64)
-        normed[pl.ds(pl.multiple_of(c * ROWS + i * 64, 64), 64), :] = norm_rows(raw[at, :], grid_gain[...]).astype(BF16)
-        return carry
-
     base = b * (8 * ROWS) + x * (2 * ROWS)
     rim_row = jnp.where(is_top, ROWS, 0)
-    local[2].wait()
-    lax.fori_loop(0, ROWS // 64, grid_block, 0)
-    rows_to_partner(grid_own).start()
     sort_edges(edges, counts, columns, base, 2 * ROWS)
     fill_bias(columns, bias, 2 * ROWS)
     weight_relay(0, 0)
     weight_relay(1, 0)
-    spread_o.spread()
     vals[:, COLS:] = jnp.ones((2 * ROWS, COLS), BF16)
     stat[...] = jnp.zeros_like(stat)
     stat_r[...] = jnp.zeros_like(stat_r)
@@ -408,6 +413,15 @@
         sort_edges(edges_r, counts_r, columns, base + rim_row, ROWS)
         fill_bias(columns, bias_r, ROWS)
 
+    for xx in others:
+        q_arrival(q, q_recv, xx).wait_recv()
+
+    @pl.when(is_rim)
+    def _():
+        for xx in others:
+            qr_copy(xx).start()
+
+    spread_o.spread()
     rows_to_partner(grid_other).wait_recv()
 
     def part_copy(xs, d):
@@ -494,15 +508,14 @@
             weight_relay(2, 0)
             weight_relay(2, 1)
 
-        q_arrival(q, q_recv, xs).wait_recv()
         slice_of(xs)
         return carry
 
     local[0].wait()
     local[1].wait()
-    slice_of(x)
     weight_relay(0, 1)
     weight_relay(1, 1)
+    slice_of(x)
     lax.fori_loop(1, 4, head_step, 0)
 
     for half in range(2):
@@ -642,7 +655,6 @@
         for xs in range(4):
             part_copy(xs, d).wait_send()
     for k in range(2):
-        qr_copy(k).wait_send()
         kv_copy(k).wait_send()
 
     @pl.when(is_rim)
@@ -650,6 +662,7 @@
         for one in edge_copies:
             one.wait_send()
         for xx in range(4):
+            qr_copy(xx).wait_send()
             rim_stat_copy(xx).wait_send()
             for xs in range(4):
                 rim_copy(xs, xx).wait_send()
@@ -663,7 +676,8 @@
 
     def mixed_second(n, carry):
         at = pl.ds(pl.multiple_of(n * 256, 256), 256)
-        out[:, at] = (latent[:, at] + half_product(heads2, pwo_all, 1 - c, at)).astype(BF16)
+        node[:, at] = (latent[:, at] + half_product(heads2, pwo_all, 1 - c, at)).astype(BF16)
+        pltpu.make_async_copy(node.at[:, at], out.at[:, at], out_sem.at[n]).start()
         return carry
 
     lax.fori_loop(0, 4, mixed_first, 0, unroll=True)
@@ -672,6 +686,9 @@
     lax.fori_loop(0, 4, mixed_second, 0, unroll=True)
 
     ring_g.drain()
+    for n in range(4):
+        at = pl.ds(n * 256, 256)
+        pltpu.make_async_copy(node.at[:, at], out.at[:, at], out_sem.at[n]).wait()
 
 
 def solution(mesh):
@@ -694,7 +711,7 @@
             functools.partial(kernel, bands, ring),
             out_shape=jax.ShapeDtypeStruct((NODES, D), BF16),
             in_specs=[hbm] * 10 + [vmem] * 7,
-            out_specs=vmem,
+            out_specs=hbm,
             scratch_shapes=[
                 pltpu.VMEM((ROWS, D), BF16),
                 pltpu.VMEM((2 * ROWS, D), BF16),
@@ -735,7 +752,8 @@
                 dma((2,)),
                 dma((2, 2)),
                 dma((3,)), dma((4,)),
-                dma((2,)), dma((4,)),
+                dma((4,)), dma((4,)),
+                dma((4,)),
                 dma((3, 4)), dma((6, 4)),
                 dma((3,)), dma((6,)),
                 dma((4, 4)), dma((4,)),

time: 83.6 us -> 82.6 us (0.988)
  Pallas kernels: 81.5 us -> 80.5 us
    pallas_call x1, Pallas kernels: 81.5 us -> 80.5 us  [step(): pl.pallas_call(functools.partial(kernel, bands, ring), out_shape=jax.Shap...]
where the time goes in v5:
time: 82.6 us; the launch traced here: 82.4 us
  Pallas kernels  80.5 us (97%)
  local copies, waits for them, and re-layouts  1.87 us (2%)
    pallas_call x1, Pallas kernels, step(): pl.pallas_call(functools.partial(kernel, bands, ring), out_shape=jax.Shap...  80.5 us
    unnamed x1, local copies, waits for them, and re-layouts  1.87 us

profile of v5, /device:TPU:1, one launch (start us, length us, event | category | flops | bytes accessed | tf_op | source)
XLA Modules:
  0.0 82.4 jit_solution(16217650878679814579)
XLA Ops:
  0.0 80.5 %shard_map.145 = bf16[256,1024]{1,0:T(8,128)(2,1)} custom-call(bf16[512,1024]{1,0:T(8,128)(2,1)} %grid.1, bf16[1024,128]{1,0:T(8,128)(2,1)} %wk.1, bf16[1024,128]{1,0:T(8,128)(2,1)} %wv.1, bf16[128,1024]{1,0:T(8,128)(2,1)} %wo.1, bf16[1024,128]{1,0:T(8,128)(2,1)} %pwk.1, bf16[1024,128]{1,0:T(8,128)(2,1)} %pwv.1, bf16[1024,128]{1,0:T(8,128)(2,1)} %pwq.1, ...), custom_call_target="tpu_custom_call" | custom-call | tf_op jit(solution)/shard_map/pallas_call | solution.py:710
  80.5 1.9 %copy.17 = bf16[256,1024]{1,0:T(8,128)(2,1)} copy(bf16[256,1024]{1,0:T(8,128)(2,1)} %shard_map.145) | data formatting | bytes 1048576

commit v6 on v5

--- a/solution.py
+++ b/solution.py
@@ -514,8 +514,8 @@
     local[0].wait()
     local[1].wait()
     weight_relay(0, 1)
+    slice_of(x)
     weight_relay(1, 1)
-    slice_of(x)
     lax.fori_loop(1, 4, head_step, 0)
 
     for half in range(2):

time: 82.6 us -> 83.3 us (level)
  no operation moved by 1% of the time
where the time goes in v6:
time: 83.3 us; the launch traced here: 83.1 us
  Pallas kernels  81.3 us (98%)
  local copies, waits for them, and re-layouts  1.87 us (2%)
    pallas_call x1, Pallas kernels, step(): pl.pallas_call(functools.partial(kernel, bands, ring), out_shape=jax.Shap...  81.3 us
    unnamed x1, local copies, waits for them, and re-layouts  1.87 us

profile of v6, /device:TPU:1, one launch (start us, length us, event | category | flops | bytes accessed | tf_op | source)
XLA Modules:
  0.0 83.1 jit_solution(16925991693890260417)
XLA Ops:
  0.0 81.3 %shard_map.145 = bf16[256,1024]{1,0:T(8,128)(2,1)} custom-call(bf16[512,1024]{1,0:T(8,128)(2,1)} %grid.1, bf16[1024,128]{1,0:T(8,128)(2,1)} %wk.1, bf16[1024,128]{1,0:T(8,128)(2,1)} %wv.1, bf16[128,1024]{1,0:T(8,128)(2,1)} %wo.1, bf16[1024,128]{1,0:T(8,128)(2,1)} %pwk.1, bf16[1024,128]{1,0:T(8,128)(2,1)} %pwv.1, bf16[1024,128]{1,0:T(8,128)(2,1)} %pwq.1, ...), custom_call_target="tpu_custom_call" | custom-call | tf_op jit(solution)/shard_map/pallas_call | solution.py:710
  81.3 1.9 %copy.17 = bf16[256,1024]{1,0:T(8,128)(2,1)} copy(bf16[256,1024]{1,0:T(8,128)(2,1)} %shard_map.145) | data formatting | bytes 1048576
